TPU v7x, 512 devices: a whole 4x8x8 slice. The times are simulated.
512 devices in a mesh: fsdp: 32 (over x, y_hi, core), tensor: 16 (over z, y_lo).
Axes of the slice: x: 4, y: 8 (y_hi: 4, y_lo: 2; y = y_hi * 2 + y_lo), z: 8, core: 2. Of those that a mesh axis runs over, the one named last changes fastest.
Arguments:
- policy_token_inputs: bfloat16 [6144, 8192], P('fsdp', 'tensor'), may hold values from -6 to 6
- reference_tokens: bfloat16 [6144, 8192], P('fsdp', 'tensor'), may hold values from -6 to 6
- cotangent: bfloat16 [6144, 4096], P('fsdp', 'tensor'), may hold values from -6 to 6
- query_weight: bfloat16 [8192, 4096], P('fsdp', 'tensor'), may hold values from -1 to 1
- key_weight: bfloat16 [8192, 512], P('fsdp', 'tensor'), may hold values from -1 to 1
- value_weight: bfloat16 [8192, 512], P('fsdp', 'tensor'), may hold values from -0.0625 to 0.0625
- query_down: bfloat16 [8192, 64], P('tensor'), may hold values from -0.0625 to 0.0625
- value_down: bfloat16 [8192, 64], P('tensor'), may hold values from -0.0625 to 0.0625
- query_raise_factor: bfloat16 [64, 4096], P(None, 'tensor'), may hold values from -0.75 to 0.75
- value_raise_factor: bfloat16 [64, 512], P(None, 'tensor'), may hold values from -0.75 to 0.75
- policy_lengths: int32 [64], P('fsdp'), may hold values from 24 to 96
- reference_lengths: int32 [64], P('fsdp'), may hold values from 24 to 96
- chosen_flags: int32 [64], P('fsdp'), may hold values from 0 to 1, as said below
- log_ratios: float32 [64], P('fsdp'), may hold values from -60 to 60
Outputs:
- reference_context: bfloat16 [6144, 4096], P('fsdp', 'tensor')
- query_down_gradient: float32 [8192, 64], P('tensor')
- value_down_gradient: float32 [8192, 64], P('tensor')
- query_up_gradient: float32 [64, 4096], P(None, 'tensor')
- value_up_gradient: float32 [64, 512], P(None, 'tensor')
Inputs may be any that keep to these rules, and one draw needn't show every extreme that they name: `chosen_flags`: sequences 2p and 2p+1 form a pair: one is 1 and the other 0. `policy_lengths`: valid tokens stand at the start of each sequence. `reference_lengths`: valid tokens stand at the start of each sequence.
All inputs are finite; a program needn't handle non-finite values.
Results may differ from a plain program's by a relative error of at most 0.007.
The roundings to bfloat16 on the way count: a program that leaves them out, or rounds other values in their place, can miss the bound.
Values may be sent and summed in bfloat16 or wider, within the bound.
A program may use at most 64 MiB of HBM per device.

v0:
```python
import math

import jax
import jax.numpy as jnp
from jax import lax
from jax.sharding import PartitionSpec as P

HD = 128
KVH = 4


ADAPTER_SCALE = 2.0
DPO_BETA = 0.1
MASKED = -1e30


def partner_2(block, axis, apart):
    count = lax.axis_size(axis)
    route = []
    for low in range(count):
        high = low | 1 << apart
        if high != low and high < count:
            route += [(low, high), (high, low)]
    return lax.ppermute(block, axis, route)


def from_everyone(value, axis):
    copies = jnp.broadcast_to(value, (lax.axis_size(axis), *value.shape))
    return lax.all_to_all(copies, axis, split_axis=0, concat_axis=0, tiled=True)


def taken_together(value, axis):
    return from_everyone(value, axis).sum(axis=0)


def together(arrays, axis):
    ends = [0]
    for a in arrays:
        ends.append(ends[-1] + a.size)
    total = taken_together(jnp.concatenate([a.ravel() for a in arrays]), axis)
    return tuple((total[b:e].reshape(a.shape) for a, b, e in zip(arrays, ends, ends[1:])))


def side_by_side(arrays, axis, dim, along):
    ends, at = ([], 0)
    for a in arrays[:-1]:
        at += a.shape[along]
        ends.append(at)
    both = jnp.concatenate(arrays, axis=along)
    return tuple(jnp.split(lax.all_gather(both, axis, axis=dim, tiled=True), ends, axis=along))


def padded_to(lines, size):
    spare = -lines.shape[0] % size
    if not spare:
        return lines
    return jnp.concatenate([lines, jnp.zeros((spare, *lines.shape[1:]), lines.dtype)])


def laid_out(blocks, dim):
    shape = list(blocks.shape[1:])
    shape[dim] *= blocks.shape[0]
    return jnp.moveaxis(blocks, 0, dim).reshape(shape)


def gather_directly(value, axis, dim):
    return laid_out(from_everyone(value, axis), dim)


def cut_along(value, dim, size):
    shape = value.shape
    blocks = value.reshape(*shape[:dim], size, shape[dim] // size, *shape[dim + 1 :])
    return jnp.moveaxis(blocks, dim, 0)


def sent_and_summed(value, axis, dim):
    size = lax.axis_size(axis)
    blocks = lax.all_to_all(cut_along(value, dim, size), axis, 0, 0, tiled=True)
    return jnp.sum(blocks, axis=0)


def total_of(value, axes):
    padded = padded_to(value, lax.axis_size(axes))
    whole = gather_directly(sent_and_summed(padded, axes, 0), axes, 0)
    return lax.slice_in_dim(whole, 0, len(value)).reshape(value.shape)


def in_one(arrays, axis):
    ends = [0]
    for a in arrays:
        ends.append(ends[-1] + a.size)
    total = total_of(jnp.concatenate([a.ravel() for a in arrays]), axis)
    return tuple((total[b:e].reshape(a.shape) for a, b, e in zip(arrays, ends, ends[1:])))


def angles(length, head_dim):
    position = jnp.arange(length).astype(jnp.float32)
    inverse = 500000.0 ** (-(jnp.arange(head_dim // 2).astype(jnp.float32) * 2.0) / head_dim)
    phase_table = position[:, None] * inverse[None, :]
    return (jnp.cos(phase_table), jnp.sin(phase_table))


def rotate(values_in, cosine, sine_table, direction):
    half_dim = values_in.shape[-1] // 2
    first_half = values_in[..., :half_dim]
    second_half = values_in[..., half_dim:]
    return jnp.concatenate(
        [
            first_half * cosine - direction * second_half * sine_table,
            second_half * cosine + direction * first_half * sine_table,
        ],
        axis=-1,
    )


def accumulate(inputs, pieces):
    updated = []
    for position, tokens in enumerate(inputs):
        for offset, weight_piece in enumerate(pieces):
            updated.append(jnp.dot(tokens, weight_piece, preferred_element_type=jnp.float32))
    return tuple(updated)


def gather_group(pieces, rounds):
    device_index = lax.axis_index("tensor")
    for bit_index in range(rounds):
        partner = partner_2(pieces, "tensor", bit_index)
        upper_half = device_index >> bit_index & 1 == 1
        pieces = tuple(
            (
                jnp.where(
                    upper_half,
                    jnp.concatenate([theirs, mine], axis=1),
                    jnp.concatenate([mine, theirs], axis=1),
                )
                for mine, theirs in zip(pieces, partner)
            )
        )
    return pieces


def reduce_group(partial_value, rounds):
    device_index = lax.axis_index("tensor")
    for bit_index in reversed(range(rounds)):
        half_width = partial_value.shape[1] // 2
        lower_half = partial_value[:, :half_width]
        upper_part = partial_value[:, half_width:]
        upper_half = device_index >> bit_index & 1 == 1
        sent_half = jnp.where(upper_half, lower_half, upper_part)
        kept_half = jnp.where(upper_half, upper_part, lower_half)
        received = partner_2(sent_half, "tensor", bit_index)
        partial_value = kept_half + received
    return partial_value


def softmax_rows(query_rows, keys_rot, lengths, score_scale):
    seq_len = query_rows.shape[1]
    scores = (
        jnp.einsum("sqhd,skd->shqk", query_rows, keys_rot, preferred_element_type=jnp.float32)
        * score_scale
    )
    positions = jnp.arange(seq_len)
    allowed = (positions[None, :] <= positions[:, None])[None] & (
        positions[None, None, :] < lengths[:, None, None]
    )
    scores = jnp.where(allowed[:, None], scores, MASKED)
    row_top = jnp.max(scores, axis=-1, keepdims=True)
    exponent = jnp.exp(scores - row_top)
    return exponent / jnp.sum(exponent, axis=-1, keepdims=True)


def shards(
    policy_token_inputs,
    reference_tokens,
    cotangent,
    query_weight,
    key_weight,
    value_weight,
    query_down,
    value_down,
    query_raise_factor,
    value_raise_factor,
    policy_lengths,
    reference_lengths,
    chosen_flags,
    log_ratios,
):
    local_seqs = policy_lengths.shape[0]
    tok_rows = policy_token_inputs.shape[0]
    seq_len = tok_rows // local_seqs
    local_heads = query_weight.shape[1] // HD
    rounds = (lax.axis_size("tensor") // KVH).bit_length() - 1
    score_scale = 1.0 / math.sqrt(HD)
    cosine, sine_table = angles(seq_len, HD)
    query_lowrank, value_lowrank = together(
        (
            jnp.dot(policy_token_inputs, query_down, preferred_element_type=jnp.float32),
            jnp.dot(policy_token_inputs, value_down, preferred_element_type=jnp.float32),
        ),
        "tensor",
    )
    query_lowrank = query_lowrank.astype(jnp.bfloat16)
    value_lowrank = value_lowrank.astype(jnp.bfloat16)
    whole_policy, whole_reference = side_by_side(
        (policy_token_inputs, reference_tokens), "tensor", 1, 0
    )
    summed = accumulate(
        (whole_policy, whole_reference),
        side_by_side((query_weight, key_weight, value_weight), "fsdp", 0, 1),
    )
    policy_frozen_output = summed[:3]
    reference_base = summed[3:]
    policy_query = policy_frozen_output[0] + ADAPTER_SCALE * jnp.dot(
        query_lowrank, query_raise_factor, preferred_element_type=jnp.float32
    )
    policy_value = policy_frozen_output[2] + ADAPTER_SCALE * jnp.dot(
        value_lowrank, value_raise_factor, preferred_element_type=jnp.float32
    )
    key_pol, value_pol, key_ref, value_ref = gather_group(
        (policy_frozen_output[1], policy_value, reference_base[1], reference_base[2]), rounds
    )

    def prepare(query_rows, keys_whole, values_whole):
        query_rows = rotate(
            query_rows.reshape(local_seqs, seq_len, local_heads, HD),
            cosine[:, None, :],
            sine_table[:, None, :],
            1.0,
        ).astype(jnp.bfloat16)
        keys_rot = rotate(
            keys_whole.reshape(local_seqs, seq_len, HD), cosine, sine_table, 1.0
        ).astype(jnp.bfloat16)
        value_rows = values_whole.astype(jnp.bfloat16).reshape(local_seqs, seq_len, HD)
        return (query_rows, keys_rot, value_rows)

    queries_ref, keys_ref, values_ref = prepare(reference_base[0], key_ref, value_ref)
    attention_ref = softmax_rows(queries_ref, keys_ref, reference_lengths, score_scale).astype(
        jnp.bfloat16
    )
    reference_context = jnp.einsum(
        "shqk,skd->sqhd", attention_ref, values_ref, preferred_element_type=jnp.float32
    )
    reference_context = reference_context.astype(jnp.bfloat16).reshape(tok_rows, local_heads * HD)
    queries_pol, keys_pol, values_pol = prepare(policy_query, key_pol, value_pol)
    attention = softmax_rows(queries_pol, keys_pol, policy_lengths, score_scale)
    attention_b = attention.astype(jnp.bfloat16)
    pair_sign = (2.0 * chosen_flags.astype(jnp.float32) - 1.0).reshape(local_seqs // 2, 2)
    margin = DPO_BETA * jnp.sum(pair_sign * log_ratios.reshape(local_seqs // 2, 2), axis=1)
    seq_scale = (-pair_sign * (DPO_BETA * jax.nn.sigmoid(-margin))[:, None]).reshape(local_seqs)
    positions = jnp.arange(seq_len)
    live_query = (positions[None, :] < policy_lengths[:, None]).astype(jnp.float32)
    factor = seq_scale[:, None] * live_query
    d_context = (
        cotangent.astype(jnp.float32).reshape(local_seqs, seq_len, local_heads, HD)
        * factor[:, :, None, None]
    ).astype(jnp.bfloat16)
    d_probs = jnp.einsum(
        "sqhd,skd->shqk", d_context, values_pol, preferred_element_type=jnp.float32
    )
    row_total = jnp.sum(attention * d_probs, axis=-1, keepdims=True)
    d_scores = (attention * (d_probs - row_total) * score_scale).astype(jnp.bfloat16)
    query_cotangent = jnp.einsum(
        "shqk,skd->sqhd", d_scores, keys_pol, preferred_element_type=jnp.float32
    )
    query_cotangent = rotate(query_cotangent, cosine[:, None, :], sine_table[:, None, :], -1.0)
    query_cotangent = query_cotangent.reshape(tok_rows, local_heads * HD).astype(jnp.bfloat16)
    d_value_head = jnp.einsum(
        "shqk,sqhd->skd", attention_b, d_context, preferred_element_type=jnp.float32
    )
    value_cotangent = reduce_group(d_value_head.reshape(tok_rows, HD), rounds).astype(jnp.bfloat16)
    contract_rows = (((0,), (0,)), ((), ()))
    contract_cols = (((1,), (1,)), ((), ()))
    query_up_gradient = ADAPTER_SCALE * lax.dot_general(
        query_lowrank, query_cotangent, contract_rows, preferred_element_type=jnp.float32
    )
    value_up_gradient = ADAPTER_SCALE * lax.dot_general(
        value_lowrank, value_cotangent, contract_rows, preferred_element_type=jnp.float32
    )
    query_input_rows, value_input_rows = together(
        (
            lax.dot_general(
                query_cotangent,
                query_raise_factor,
                contract_cols,
                preferred_element_type=jnp.float32,
            ),
            lax.dot_general(
                value_cotangent,
                value_raise_factor,
                contract_cols,
                preferred_element_type=jnp.float32,
            ),
        ),
        "tensor",
    )
    query_input_rows = query_input_rows.astype(jnp.bfloat16)
    value_input_rows = value_input_rows.astype(jnp.bfloat16)
    query_down_gradient = ADAPTER_SCALE * lax.dot_general(
        policy_token_inputs, query_input_rows, contract_rows, preferred_element_type=jnp.float32
    )
    value_down_gradient = ADAPTER_SCALE * lax.dot_general(
        policy_token_inputs, value_input_rows, contract_rows, preferred_element_type=jnp.float32
    )
    query_down_gradient, value_down_gradient, query_up_gradient, value_up_gradient = in_one(
        (query_down_gradient, value_down_gradient, query_up_gradient, value_up_gradient), "fsdp"
    )
    return (
        reference_context,
        query_down_gradient,
        value_down_gradient,
        query_up_gradient,
        value_up_gradient,
    )


def solution(mesh):
    return jax.shard_map(
        shards,
        mesh=mesh,
        in_specs=(
            P("fsdp", "tensor"),
            P("fsdp", "tensor"),
            P("fsdp", "tensor"),
            P("fsdp", "tensor"),
            P("fsdp", "tensor"),
            P("fsdp", "tensor"),
            P("tensor", None),
            P("tensor", None),
            P(None, "tensor"),
            P(None, "tensor"),
            P("fsdp"),
            P("fsdp"),
            P("fsdp"),
            P("fsdp"),
        ),
        out_specs=(
            P("fsdp", "tensor"),
            P("tensor", None),
            P("tensor", None),
            P(None, "tensor"),
            P(None, "tensor"),
        ),
        check_vma=False,
    )
```

profile of v0, /device:TPU:1, one launch (start us, length us, event | category | flops | bytes accessed | tf_op | source)
XLA Modules:
  0.0 403.9 jit_solution(6839402985295575735)
XLA Ops:
  7.3 0.9 copy.181
  8.1 0.8 copy.182
  9.0 1.7 pad_maximum_fusion.2
  10.7 1.8 pad_maximum_fusion
  12.6 1.1 fusion.105
  13.8 1.1 fusion.106
  15.0 2.4 broadcast_in_dim.27
  17.4 12.0 %all-to-all-start = ((f32[16,1,24576]{2,1,0:T(1,128)}), f32[16,1,24576]{2,1,0:T(1,128)S(1)}, u32[]{:S(2)}, u32[]{:S(2)}) async-start(f32[16,1,24576]{2,1,0:T(1,128)} %broadcast_in_dim.27), calls=%async_computation | async-start | bytes 3145728 | tf_op jit(solution)/shard_map/all_to_all | solution.py:29
  29.4 0.6 multiply_reduce_fusion.1
  31.2 0.3 broadcast_multiply_fusion
  31.4 34.3 %all-to-all-done = f32[16,1,24576]{2,1,0:T(1,128)S(1)} async-done(((f32[16,1,24576]{2,1,0:T(1,128)}), f32[16,1,24576]{2,1,0:T(1,128)S(1)}, u32[]{:S(2)}, u32[]{:S(2)}) %all-to-all-start) | async-done | bytes 1572896 | tf_op jit(solution)/shard_map/all_to_all | solution.py:29
  65.7 1.5 reduce_sum.64
  67.4 26.1 %all-gather.5.cloned.1.call-done = bf16[8192,320]{1,0:T(8,128)(2,1)} async-done(((bf16[256,320]{1,0:T(8,128)(2,1)}), bf16[8192,320]{1,0:T(8,128)(2,1)}) %all-gather.5.cloned.1.call-update) | async-done | bytes 5242896 | tf_op jit(solution)/shard_map/all_gather | solution.py:50
  93.5 145.4 %all-gather.3.cloned.1.call-done = bf16[384,8192]{1,0:T(8,128)(2,1)} async-done(((bf16[384,512]{1,0:T(8,128)(2,1)}), bf16[384,8192]{1,0:T(8,128)(2,1)}) %all-gather.3.cloned.1.call-update) | async-done | bytes 6291472 | tf_op jit(solution)/shard_map/all_gather | solution.py:50
  238.8 4.7 %fusion.15 = bf16[192,32]{0,1:T(8,128)(2,1)S(1)} fusion(bf16[384,8192]{1,0:T(8,128)(2,1)} %all-gather.3.cloned.1.call-done, bf16[8192,320]{1,0:T(8,128)(2,1)} %all-gather.5.cloned.1.call-done), kind=kOutput, calls=%fused_computation.15 | convolution fusion | flops 100663296 | bytes 5255168 | tf_op jit(solution)/shard_map/dot_general | solution.py:120
  243.5 1.9 collective-permute-start
  245.4 3.7 fusion.13
  249.1 3.4 collective-permute-start.2
  252.5 3.0 fusion.5
  255.6 4.1 %fusion.3 = f32[192,256]{1,0:T(8,128)S(1)} fusion(bf16[8192,320]{1,0:T(8,128)(2,1)} %all-gather.5.cloned.1.call-done, bf16[384,8192]{1,0:T(8,128)(2,1)} %all-gather.3.cloned.1.call-done), kind=kOutput, calls=%fused_computation.3 | convolution fusion | flops 805306368 | bytes 7536640 | tf_op jit(solution)/shard_map/dot_general | solution.py:120
  260.1 4.5 %fusion.7 = f32[192,32]{0,1:T(8,128)S(1)} fusion(bf16[384,8192]{1,0:T(8,128)(2,1)} %all-gather.3.cloned.1.call-done, bf16[8192,320]{1,0:T(8,128)(2,1)} %all-gather.5.cloned.1.call-done), kind=kOutput, calls=%fused_computation.7 | convolution fusion | flops 100663296 | bytes 5267456 | tf_op jit(solution)/shard_map/dot_general | solution.py:120
  264.8 1.9 collective-permute-start.6
  266.7 0.5 fusion.95
  267.2 3.7 fusion.10
  271.2 3.4 collective-permute-start.4
  274.9 1.9 collective-permute-start.7
  277.2 3.4 collective-permute-start.5
  280.6 2.1 collective-permute-start.3
  283.2 0.3 convolution_bitcast_fusion.1
  283.7 2.1 collective-permute-done.3
  286.1 0.3 fusion.102
  286.5 0.5 fusion.53
  287.1 1.9 collective-permute-start.8
  289.0 0.3 convolution_bitcast_fusion
  289.6 2.8 collective-permute-done.8
  292.7 2.7 collective-permute-start.9
  295.6 2.4 collective-permute-done.9
  298.3 2.4 broadcast_in_dim.28
  300.7 5.3 %all-to-all-start.1 = ((f32[16,1,24576]{2,1,0:T(1,128)}), f32[16,1,24576]{2,1,0:T(1,128)S(1)}, u32[]{:S(2)}, u32[]{:S(2)}) async-start(f32[16,1,24576]{2,1,0:T(1,128)} %broadcast_in_dim.28), calls=%async_computation.1 | async-start | bytes 3145728 | tf_op jit(solution)/shard_map/all_to_all | solution.py:29
  306.2 0.2 convolution_multiply_fusion.7
  306.5 36.1 %all-to-all-done.1 = f32[16,1,24576]{2,1,0:T(1,128)S(1)} async-done(((f32[16,1,24576]{2,1,0:T(1,128)}), f32[16,1,24576]{2,1,0:T(1,128)S(1)}, u32[]{:S(2)}, u32[]{:S(2)}) %all-to-all-start.1) | async-done | bytes 1572896 | tf_op jit(solution)/shard_map/all_to_all | solution.py:29
  342.6 1.5 reduce_sum.68
  344.3 0.2 fusion.34
  344.5 0.2 fusion.35
  345.2 0.4 all_to_all.20
  345.6 26.4 %all_to_all.27 = f32[32,1,2624]{2,1,0:T(1,128)S(1)} all-to-all(f32[32,1,2624]{2,1,0:T(1,128)S(1)} %all_to_all.20), channel_id=1, replica_groups=mesh['fsdp'=32,'tensor'=16] {'fsdp'}, dimensions={0} | all-to-all | bytes 671744 | tf_op jit(solution)/shard_map/all_to_all | solution.py:78
  372.0 0.2 reduce_sum.69
  372.2 0.9 broadcast_in_dim.29
  373.1 4.8 %all-to-all-start.3 = ((f32[32,1,2624]{2,1,0:T(1,128)}), f32[32,1,2624]{2,1,0:T(1,128)S(1)}, u32[]{:S(2)}, u32[]{:S(2)}) async-start(f32[32,1,2624]{2,1,0:T(1,128)} %broadcast_in_dim.29), calls=%async_computation.3 | async-start | bytes 688128 | tf_op jit(solution)/shard_map/all_to_all | solution.py:29
  378.0 2.3 collective-permute-start.1
  380.3 2.6 collective-permute-done.1
  383.0 0.4 fusion.99
  383.4 0.3 fusion.27
  383.7 0.3 fusion.36
  384.1 0.7 copy.282
  384.7 7.6 %all-to-all-done.3 = f32[32,1,2624]{2,1,0:T(1,128)S(1)} async-done(((f32[32,1,2624]{2,1,0:T(1,128)}), f32[32,1,2624]{2,1,0:T(1,128)S(1)}, u32[]{:S(2)}, u32[]{:S(2)}) %all-to-all-start.3) | async-done | bytes 335904 | tf_op jit(solution)/shard_map/all_to_all | solution.py:29
  392.3 0.8 reduce.5
  393.1 0.2 slice.133
  393.4 0.2 slice.130
  393.6 0.5 slice.135
  394.1 0.6 slice.157
  394.8 0.8 copy.226
  395.6 0.8 copy.225
  396.3 0.7 copy.227
  (97 shorter events, 5.8 us)
Async XLA Ops:
  7.2 5.4 %copy-start = (bf16[512,64]{0,1:T(8,128)(2,1)S(1)}, bf16[512,64]{0,1:T(8,128)(2,1)}, u32[]{:S(2)}) copy-start(bf16[512,64]{0,1:T(8,128)(2,1)} %param.20) | copy-start | bytes 196612
  7.2 22.2 %copy-start.9 = (s32[2]{0:T(128)S(1)}, s32[2]{0:T(128)}, u32[]{:S(2)}) copy-start(s32[2]{0:T(128)} %param.26) | copy-start | bytes 28
  7.2 22.2 %copy-start.8 = (f32[2]{0:T(128)S(1)}, f32[2]{0:T(128)}, u32[]{:S(2)}) copy-start(f32[2]{0:T(128)} %param.27) | copy-start | bytes 28
  7.2 23.5 %copy-start.3 = (bf16[192,256]{1,0:T(8,128)(2,1)S(1)}, bf16[192,256]{1,0:T(8,128)(2,1)}, u32[]{:S(2)}) copy-start(bf16[192,256]{1,0:T(8,128)(2,1)} %param.16) | copy-start | bytes 294916
  7.2 23.7 %copy-start.5 = (s32[2]{0:T(128)S(1)}, s32[2]{0:T(128)}, u32[]{:S(2)}) copy-start(s32[2]{0:T(128)} %param.24) | copy-start | bytes 28
  7.2 23.8 %copy-start.6 = (s32[2]{0:T(128)S(1)}, s32[2]{0:T(128)}, u32[]{:S(2)}) copy-start(s32[2]{0:T(128)} %param.25) | copy-start | bytes 28
  7.2 86.2 %all-gather.5.cloned.1.call-start = ((), (), s32[]{:S(2)}) async-start(), calls=%async_computation.5 | async-start | bytes 6488064 | tf_op jit(solution)/shard_map/all_gather | solution.py:50
  10.7 228.1 %all-gather.3.cloned.1.call-start = ((), (), s32[]{:S(2)}) async-start(), calls=%async_computation.4 | async-start | bytes 6684672 | tf_op jit(solution)/shard_map/all_gather | solution.py:50
  17.4 48.3 %all-to-all-start = ((f32[16,1,24576]{2,1,0:T(1,128)}), f32[16,1,24576]{2,1,0:T(1,128)S(1)}, u32[]{:S(2)}, u32[]{:S(2)}) async-start(f32[16,1,24576]{2,1,0:T(1,128)} %broadcast_in_dim.27), calls=%async_computation | async-start | bytes 3145728 | tf_op jit(solution)/shard_map/all_to_all | solution.py:29
  238.8 13.7 %copy-start.7 = (bf16[8192,320]{1,0:T(8,128)(2,1)S(1)}, bf16[8192,320]{1,0:T(8,128)(2,1)}, u32[]{:S(2)}) copy-start(bf16[8192,320]{1,0:T(8,128)(2,1)} %all-gather.5.cloned.1.call-done) | copy-start | bytes 15728644
  243.5 33.4 %collective-permute-start = (bf16[192,32]{0,1:T(8,128)(2,1)S(1)}, bf16[192,32]{0,1:T(8,128)(2,1)S(1)}, u32[]{:S(2)}, u32[]{:S(2)}) collective-permute-start(bf16[192,32]{0,1:T(8,128)(2,1)S(1)} %fusion.15), channel_id=1, source_target_pairs={{0,1},{1,0},{2,3},{3,2},{4,5},{5,4},{6,7},{7,6},{8,9},{9,8},{10,11... | collective-permute-start | bytes 36872 | tf_op jit(solution)/shard_map/ppermute | solution.py:24
  249.1 31.4 %collective-permute-start.2 = (f32[192,32]{0,1:T(8,128)S(1)}, f32[192,32]{0,1:T(8,128)S(1)}, u32[]{:S(2)}, u32[]{:S(2)}) collective-permute-start(f32[192,32]{0,1:T(8,128)S(1)} %fusion.13), channel_id=1, source_target_pairs={{0,1},{1,0},{2,3},{3,2},{4,5},{5,4},{6,7},{7,6},{8,9},{9,8},{10,11... | collective-permute-start | bytes 73736 | tf_op jit(solution)/shard_map/ppermute | solution.py:24
  255.6 4.2 %copy-start.2 = (bf16[64,256]{1,0:T(8,128)(2,1)S(1)}, bf16[64,256]{1,0:T(8,128)(2,1)}, u32[]{:S(2)}) copy-start(bf16[64,256]{1,0:T(8,128)(2,1)} %param.22) | copy-start | bytes 98308
  259.8 4.8 %copy-start.4 = (bf16[64,32]{0,1:T(8,128)(2,1)S(1)}, bf16[64,32]{0,1:T(8,128)(2,1)}, u32[]{:S(2)}) copy-start(bf16[64,32]{0,1:T(8,128)(2,1)} %param.23) | copy-start | bytes 12292
  264.8 10.1 %collective-permute-start.6 = (bf16[192,32]{0,1:T(8,128)(2,1)S(1)}, bf16[192,32]{0,1:T(8,128)(2,1)S(1)}, u32[]{:S(2)}, u32[]{:S(2)}) collective-permute-start(bf16[192,32]{0,1:T(8,128)(2,1)S(1)} %fusion.38), channel_id=1, source_target_pairs={{0,1},{1,0},{2,3},{3,2},{4,5},{5,4},{6,7},{7,6},{8,9},{9,8},{10,11... | collective-permute-start | bytes 36872 | tf_op jit(solution)/shard_map/ppermute | solution.py:24
  271.2 5.9 %collective-permute-start.4 = (f32[192,32]{0,1:T(8,128)S(1)}, f32[192,32]{0,1:T(8,128)S(1)}, u32[]{:S(2)}, u32[]{:S(2)}) collective-permute-start(f32[192,32]{0,1:T(8,128)S(1)} %fusion.10), channel_id=1, source_target_pairs={{0,1},{1,0},{2,3},{3,2},{4,5},{5,4},{6,7},{7,6},{8,9},{9,8},{10,11... | collective-permute-start | bytes 73736 | tf_op jit(solution)/shard_map/ppermute | solution.py:24
  274.9 8.2 %collective-permute-start.7 = (bf16[192,64]{0,1:T(8,128)(2,1)S(1)}, bf16[192,64]{0,1:T(8,128)(2,1)S(1)}, u32[]{:S(2)}, u32[]{:S(2)}) collective-permute-start(bf16[192,64]{0,1:T(8,128)(2,1)S(1)} %maximum_select_fusion.11), channel_id=1, source_target_pairs={{0,2},{2,0},{1,3},{3,1},{4,6},{6,4},{5,7},{7,5},{8,10},{10,8},{9,1... | collective-permute-start | bytes 73736 | tf_op jit(solution)/shard_map/ppermute | solution.py:24
  277.2 6.3 %collective-permute-start.5 = (f32[192,64]{0,1:T(8,128)S(1)}, f32[192,64]{0,1:T(8,128)S(1)}, u32[]{:S(2)}, u32[]{:S(2)}) collective-permute-start(f32[192,64]{0,1:T(8,128)S(1)} %maximum_select_fusion.10), channel_id=1, source_target_pairs={{0,2},{2,0},{1,3},{3,1},{4,6},{6,4},{5,7},{7,5},{8,10},{10,8},{9,1... | collective-permute-start | bytes 147464 | tf_op jit(solution)/shard_map/ppermute | solution.py:24
  280.6 5.2 %collective-permute-start.3 = (f32[192,64]{0,1:T(8,128)S(1)}, f32[192,64]{0,1:T(8,128)S(1)}, u32[]{:S(2)}, u32[]{:S(2)}) collective-permute-start(f32[192,64]{0,1:T(8,128)S(1)} %maximum_select_fusion.9), channel_id=1, source_target_pairs={{0,2},{2,0},{1,3},{3,1},{4,6},{6,4},{5,7},{7,5},{8,10},{10,8},{9,1... | collective-permute-start | bytes 147464 | tf_op jit(solution)/shard_map/ppermute | solution.py:24
  287.1 5.4 %collective-permute-start.8 = (f32[192,64]{1,0:T(8,128)S(1)}, f32[192,64]{1,0:T(8,128)S(1)}, u32[]{:S(2)}, u32[]{:S(2)}) collective-permute-start(f32[192,64]{1,0:T(8,128)S(1)} %slice_select_fusion.1), channel_id=1, source_target_pairs={{0,2},{2,0},{1,3},{3,1},{4,6},{6,4},{5,7},{7,5},{8,10},{10,8},{9,1... | collective-permute-start | bytes 147464 | tf_op jit(solution)/shard_map/ppermute | solution.py:24
  292.7 5.4 %collective-permute-start.9 = (f32[192,32]{1,0:T(8,128)S(1)}, f32[192,32]{1,0:T(8,128)S(1)}, u32[]{:S(2)}, u32[]{:S(2)}) collective-permute-start(f32[192,32]{1,0:T(8,128)S(1)} %slice_select_fusion), channel_id=1, source_target_pairs={{0,1},{1,0},{2,3},{3,2},{4,5},{5,4},{6,7},{7,6},{8,9},{9,8},{10,11... | collective-permute-start | bytes 73736 | tf_op jit(solution)/shard_map/ppermute | solution.py:24
  295.4 48.9 %copy-start.1 = (bf16[192,512]{1,0:T(8,128)(2,1)S(1)}, bf16[192,512]{1,0:T(8,128)(2,1)}, u32[]{:S(2)}) copy-start(bf16[192,512]{1,0:T(8,128)(2,1)} %param.14) | copy-start | bytes 589828
  300.7 41.9 %all-to-all-start.1 = ((f32[16,1,24576]{2,1,0:T(1,128)}), f32[16,1,24576]{2,1,0:T(1,128)S(1)}, u32[]{:S(2)}, u32[]{:S(2)}) async-start(f32[16,1,24576]{2,1,0:T(1,128)} %broadcast_in_dim.28), calls=%async_computation.1 | async-start | bytes 3145728 | tf_op jit(solution)/shard_map/all_to_all | solution.py:29
  373.1 19.2 %all-to-all-start.3 = ((f32[32,1,2624]{2,1,0:T(1,128)}), f32[32,1,2624]{2,1,0:T(1,128)S(1)}, u32[]{:S(2)}, u32[]{:S(2)}) async-start(f32[32,1,2624]{2,1,0:T(1,128)} %broadcast_in_dim.29), calls=%async_computation.3 | async-start | bytes 688128 | tf_op jit(solution)/shard_map/all_to_all | solution.py:29
  378.0 5.0 %collective-permute-start.1 = (bf16[192,64]{0,1:T(8,128)(2,1)S(1)}, bf16[192,64]{0,1:T(8,128)(2,1)S(1)}, u32[]{:S(2)}, u32[]{:S(2)}) collective-permute-start(bf16[192,64]{0,1:T(8,128)(2,1)S(1)} %maximum_select_fusion.8), channel_id=1, source_target_pairs={{0,2},{2,0},{1,3},{3,1},{4,6},{6,4},{5,7},{7,5},{8,10},{10,8},{9,1... | collective-permute-start | bytes 73736 | tf_op jit(solution)/shard_map/ppermute | solution.py:24
Sparse Core Ops, SparseCore 0:
  11.2 82.2 all-gather.4
  95.5 143.2 all-gather.2
where the time goes:
time: 405 us; the launch traced here: 404 us
  waiting for transfers between devices  259 us (64%)
  starting transfers between devices  47.1 us (12%)
  matrix products  29.6 us (7%)
  blocking collectives  26.4 us (7%)
  local copies, waits for them, and re-layouts  15.9 us (4%)
  between operations  15.5 us (4%)
  other arithmetic  10 us (2%)
    all_gather x2, waiting for transfers between devices, side_by_side(): lax.all_gather(both, axis, axis=dim, tiled=True)  171 us
    all_to_all x3, waiting for transfers between devices, from_everyone(): return lax.all_to_all(copies, axis, split_axis=0, concat_axis=0, tiled=True)  77.9 us
    all_to_all x1, blocking collectives, sent_and_summed(): blocks = lax.all_to_all(cut_along(value, dim, size), axis, 0, 0, tiled=True)  26.4 us
    ppermute x10, starting transfers between devices, partner_2(): return lax.ppermute(block, axis, route)  24.9 us
    dot_general x6, matrix products, accumulate(): jnp.dot(tokens, weight_piece, preferred_element_type=jnp.float32)  23.7 us
    all_to_all x3, starting transfers between devices, from_everyone(): return lax.all_to_all(copies, axis, split_axis=0, concat_axis=0, tiled=True)  22.1 us
    ppermute x10, waiting for transfers between devices, partner_2(): return lax.ppermute(block, axis, route)  9.93 us
  transfers between devices with their start and end apart: 15, of which 9 were waited for; matrix products, arithmetic and copies ran while one was open for 9% of the time, Pallas kernels for 0%

commit v1 on v0

v1 whole, which is shorter than its diff:
```python
import math

import jax
import jax.numpy as jnp
import numpy as np
from jax import lax
from jax.experimental import pallas as pl
from jax.experimental.pallas import tpu as pltpu
from jax.sharding import PartitionSpec as P

HD = 128
SEQ = 96
TOK = 192
MASKED = -1e30
F32 = jnp.float32
BF16 = jnp.bfloat16
MESH = pl.DeviceIdType.MESH
VM = pl.BlockSpec(memory_space=pltpu.VMEM)
SM = pl.BlockSpec(memory_space=pltpu.SMEM)
NT = 16
NF = 32


def dot(a, b):
    return jnp.dot(a, b, preferred_element_type=F32)


def dot_nt(a, b):
    return lax.dot_general(a, b, (((1,), (1,)), ((), ())), preferred_element_type=F32)


def dot_tn(a, b):
    return lax.dot_general(a, b, (((0,), (0,)), ((), ())), preferred_element_type=F32)


class Place:
    def __init__(self):
        self.f = lax.axis_index("fsdp")
        self.t = lax.axis_index("tensor")
        self.c = lax.rem(self.f, 2)
        self.yh = lax.rem(self.f // 2, 4)
        self.x = self.f // 8
        self.yl = lax.rem(self.t, 2)
        self.z = self.t // 2

    def at(self, x=None, yh=None, c=None, z=None, yl=None):
        x = self.x if x is None else x
        yh = self.yh if yh is None else yh
        c = self.c if c is None else c
        z = self.z if z is None else z
        yl = self.yl if yl is None else yl
        return ((x * 4 + yh) * 2 + c, z * 2 + yl)


class Wires:
    def __init__(self, send, recv):
        self.send, self.recv = send, recv
        self.sent, self.got, self.pending = 0, 0, []

    def slots(self, count):
        base = self.got
        self.got += count
        return base

    def copy(self, src, dst, slot, device, start=True):
        copy = pltpu.make_async_remote_copy(
            src_ref=src,
            dst_ref=dst,
            send_sem=self.send.at[self.sent],
            recv_sem=self.recv.at[slot],
            device_id=device,
            device_id_type=MESH,
        )
        self.sent += 1
        if start:
            copy.start()
            self.pending.append(copy)
        return copy

    def arrived(self, dst, slot, device):
        pltpu.make_async_remote_copy(
            src_ref=dst,
            dst_ref=dst,
            send_sem=self.send.at[0],
            recv_sem=self.recv.at[slot],
            device_id=device,
            device_id_type=MESH,
        ).wait_recv()

    def drain(self):
        for copy in self.pending:
            copy.wait_send()


def greet(devices):
    barrier = pltpu.get_barrier_semaphore()
    for device in devices:
        pl.semaphore_signal(barrier, inc=1, device_id=device, device_id_type=MESH)
    return len(devices)


def met(count):
    pl.semaphore_wait(pltpu.get_barrier_semaphore(), count)


def group_peers(me, axis):
    if axis == "tensor":
        return [(me.f, lax.rem(me.t + d, NT)) for d in range(1, NT)]
    return [(lax.rem(me.f + d, NF), me.t) for d in range(1, NF)]


def scatter_start(wires, me, axis, pieces, landing):
    mine = me.t if axis == "tensor" else me.f
    peers = group_peers(me, axis)
    base = wires.slots(len(peers))
    for d, peer in enumerate(peers):
        to = peer[1] if axis == "tensor" else peer[0]
        wires.copy(pieces.at[to], landing.at[mine], base + d, peer)
    landing[mine] = pieces[mine]
    return base


def scatter_sum(wires, me, axis, landing, base):
    size = NT if axis == "tensor" else NF
    mine = me.t if axis == "tensor" else me.f
    for d in range(1, size):
        source = lax.rem(mine + size - d, size)
        wires.arrived(landing.at[source], base + d - 1, (me.f, me.t))
    total = landing[0]
    for i in range(1, size):
        total = total + landing[i]
    return total


def gather_start(wires, me, axis, blocks):
    mine = me.t if axis == "tensor" else me.f
    peers = group_peers(me, axis)
    base = wires.slots(len(peers))
    for d, peer in enumerate(peers):
        wires.copy(blocks.at[mine], blocks.at[mine], base + d, peer)
    return base


def gather_wait(wires, me, axis, blocks, base):
    size = NT if axis == "tensor" else NF
    mine = me.t if axis == "tensor" else me.f
    for d in range(1, size):
        source = lax.rem(mine + size - d, size)
        wires.arrived(blocks.at[source], base + d - 1, (me.f, me.t))


def project(
    xp, xr, wq, kvx, down, rq,
    qp, kvp, qr, kvr, low, rkv,
    xg, wgq, wgkv, kvt, kvb, flat, lows, lowl, lowg,
    part, sb, rb, ye, send, recv, local,
):
    me = Place()
    c, z, x, yh, yl = me.c, me.z, me.x, me.yh, me.yl
    wires = Wires(send, recv)
    sibling = me.at(c=1 - c)
    ypair = me.at(yl=1 - yl)
    zpair = me.at(z=z + 1 - 2 * lax.rem(z, 2))
    zs = (me.at(z=lax.rem(z + 1, 8)), me.at(z=lax.rem(z + 7, 8)))
    xs = (me.at(x=lax.rem(x + 1, 4)), me.at(x=lax.rem(x + 3, 4)))
    ring = [me.at(yh=lax.rem(yh + d, 4), yl=v) for d in range(1, 4) for v in range(2)]
    count = greet(group_peers(me, "tensor") + [sibling, *xs, *ring])

    def rows(o):
        return pl.ds(pl.multiple_of((c if o == 0 else 1 - c) * TOK, TOK), TOK)

    def features(block):
        return pl.ds(pl.multiple_of(block * 256, 256), 256)

    def xblock(kind, o, zz):
        return xg.at[kind, rows(o), features(zz)]

    def half(ref, which):
        return ref.at[:, features(which)]

    inputs = (xp, xr)
    own = []
    for kind in range(2):
        own.append(pltpu.make_async_copy(half(inputs[kind], c), xblock(kind, 0, z), local.at[kind]))
        own[-1].start()
    met(count)

    yl_d = lax.rem(yh, 2)
    m_own = yh // 2

    def wrows(xx, m):
        return pl.ds(pl.multiple_of((2 * xx + m) * 256, 256), 256)

    def wslot(ref, v, xx, m):
        return ref.at[v, wrows(xx, m)]

    maybe = []

    def y_sends(src, ref, base):
        dst = wslot(ref, yl, x, m_own)
        slot = base + m_own * 2 + yl
        near = wires.copy(src, dst, slot, me.at(yl=yl_d), start=False)
        maybe.append(near)

        @pl.when(yl == yl_d)
        def _():
            pltpu.make_async_copy(src, dst, recv.at[slot]).start()

        @pl.when(yl != yl_d)
        def _():
            near.start()

        for d in (1, 3, 2):
            wires.copy(src, dst, slot, me.at(yh=lax.rem(yh + d, 4), yl=yl_d))

    yq, ykv = wires.slots(4), wires.slots(4)
    y_sends(wq, wgq, yq)
    kz = wires.slots(1)
    wires.copy(kvx, kvt, kz, zpair)
    sib = wires.slots(2)

    def sib_send(kind):
        wires.copy(half(inputs[kind], 1 - c), xblock(kind, 0, z), sib + kind, sibling)

    zbase = wires.slots(2 * 2 * 2 * 4)

    def zidx(kind, o, way, s):
        return zbase + ((kind * 2 + o) * 2 + way) * 4 + s - 1

    def zblock(way, s):
        return lax.rem(z + (8 - s if way == 0 else s), 8)

    def zlast(o, way):
        return 4 if o == way else 3

    def zsend(kind, o, way, s):
        if s > zlast(o, way):
            return
        block = zblock(way, s - 1)
        src = half(inputs[kind], c) if (s == 1 and o == 0) else xblock(kind, o, block)
        wires.copy(src, xblock(kind, o, block), zidx(kind, o, way, s), zs[way])

    def zstep(kind, s):
        for o in range(2):
            for way in range(2):
                if s <= zlast(o, way):
                    wires.arrived(xblock(kind, o, zblock(way, s)), zidx(kind, o, way, s), zs[way])
                    zsend(kind, o, way, s + 1)

    sib_send(0)
    zsend(0, 0, 0, 1)
    zsend(0, 0, 1, 1)
    sib_send(1)

    wires.arrived(kvt, kz, zpair)
    even = lax.rem(z, 2) == 0
    mine, theirs = kvx[...], kvt[...]
    kvb[...] = jnp.where(
        even,
        jnp.concatenate([mine, theirs], axis=1).astype(F32),
        jnp.concatenate([theirs, mine], axis=1).astype(F32),
    ).astype(BF16)
    y_sends(kvb.at[pl.ds(0, 256)], wgkv, ykv)
    ry = wires.slots(1)
    raise_rows = kvb.at[pl.ds(256, 64)]
    wires.copy(raise_rows, rkv.at[yl], ry, ypair)
    rkv[yl] = kvb[pl.ds(256, 64), :]

    wires.arrived(xblock(0, 1, z), sib, sibling)
    zsend(0, 1, 0, 1)
    zsend(0, 1, 1, 1)

    flat[...] = dot(xp[...], down[...])
    for i in range(NT):
        lows[i] = flat[pl.ds(12 * i, 12), :]
    lbase = scatter_start(wires, me, "tensor", lows, lowl)

    xbase = wires.slots(2 * 4 * 2 * 2)
    refs = (wgq, wgkv)
    ybases = (yq, ykv)
    order = [(m_own, yl), (m_own, 1 - yl), (1 - m_own, yl), (1 - m_own, 1 - yl)]

    def xidx(which, j, way, s):
        return xbase + ((which * 4 + j) * 2 + way) * 2 + s - 1

    def xfrom(way, s):
        return lax.rem(x + (4 - s if way == 0 else s), 4)

    def ystep(which, j):
        m, v = order[j]
        block = wslot(refs[which], v, x, m)
        wires.arrived(block, ybases[which] + m * 2 + v, ypair)
        for way in range(2):
            wires.copy(block, block, xidx(which, j, way, 1), xs[way])

    def xwait(which, j, way, s):
        m, v = order[j]
        block = wslot(refs[which], v, xfrom(way, s), m)
        wires.arrived(block, xidx(which, j, way, s), xs[way])
        return block

    def xstep(which, j):
        for way in range(2):
            block = xwait(which, j, way, 1)
            if way == j % 2:
                wires.copy(block, block, xidx(which, j, way, 2), xs[way])

    ystep(0, 0)
    ystep(0, 1)
    zstep(0, 1)
    ystep(1, 0)
    xstep(0, 0)
    ystep(0, 2)
    ystep(1, 1)
    xstep(0, 1)
    zstep(0, 2)
    ystep(0, 3)
    piece = scatter_sum(wires, me, "tensor", lowl, lbase)
    lowg[me.t] = piece
    gbase = gather_start(wires, me, "tensor", lowg)
    for o in range(2):
        if o == 1:
            wires.arrived(xblock(1, 1, z), sib + 1, sibling)
        zsend(1, o, 0, 1)
        zsend(1, o, 1, 1)
    xstep(0, 2)
    ystep(1, 2)
    xstep(1, 0)
    zstep(0, 3)
    xstep(0, 3)
    ystep(1, 3)
    xstep(1, 1)
    zstep(1, 1)
    xstep(1, 2)
    zstep(0, 4)
    xstep(1, 3)
    gather_wait(wires, me, "tensor", lowg, gbase)
    for i in range(NT):
        flat[pl.ds(12 * i, 12), :] = lowg[i]
    low[...] = flat[...].astype(BF16)
    zstep(1, 2)
    for which in range(2):
        for j in range(4):
            xwait(which, j, j % 2, 2)
    for copy in own:
        copy.wait()
    zstep(1, 3)

    pbase, ebase = wires.slots(6), wires.slots(4)

    def partials(kind):
        tokens = xg.at[kind]
        kept = rows(0)
        given = rows(1)
        for g in range(3):
            if g == 0:
                for v in range(2):
                    whole = pl.ds(v * 128, 128)
                    part[kind, g, :, whole] = dot(tokens[kept, :], wgkv[v])
                    sb[kind, g, :, whole] = dot(tokens[given, :], wgkv[v])
            else:
                weight = wgq.at[1 - yl if g == 1 else yl]
                sb[kind, g] = dot(tokens[given, :], weight[...])
                part[kind, g] = dot(tokens[kept, :], weight[...])
            wires.copy(sb.at[kind, g], rb.at[kind, g], pbase + kind * 3 + g, sibling)

    def adapter(cols, matrix):
        return 2.0 * dot(low[:, cols], matrix)

    def exchange(kind):
        for g in range(2):
            wires.arrived(rb.at[kind, g], pbase + kind * 3 + g, sibling)
            part[kind, g] = part[kind, g] + rb[kind, g]
            if kind == 0 and g == 0:
                extra = adapter(pl.ds(64, 64), kvb[pl.ds(256, 64), :])
                for v in range(2):
                    whole = pl.ds(v * 128, 128)
                    part[kind, g, :, whole] = part[kind, g, :, whole] + jnp.where(yl == v, extra, 0.0)
            wires.copy(part.at[kind, g], ye.at[kind, g], ebase + kind * 2 + g, ypair)
        wires.arrived(rb.at[kind, 2], pbase + kind * 3 + 2, sibling)
        part[kind, 2] = part[kind, 2] + rb[kind, 2]

    def finish(kind, query, keyvalue):
        wires.arrived(ye.at[kind, 0], ebase + kind * 2, ypair)
        both = part[kind, 0] + ye[kind, 0]
        keyvalue[0] = both[:, :128]
        keyvalue[1] = both[:, 128:]
        wires.arrived(ye.at[kind, 1], ebase + kind * 2 + 1, ypair)
        total = part[kind, 2] + ye[kind, 1]
        if kind == 0:
            total = total + adapter(pl.ds(0, 64), rq[...])
        query[...] = total

    partials(0)
    zstep(1, 4)
    exchange(0)
    partials(1)
    finish(0, qp, kvp)
    exchange(1)
    finish(1, qr, kvr)
    wires.arrived(rkv.at[1 - yl], ry, ypair)
    for near in maybe:

        @pl.when(yl != yl_d)
        def _(near=near):
            near.wait_send()

    wires.drain()


def lanes(shape):
    return lax.broadcasted_iota(jnp.int32, shape, len(shape) - 1)


def sublanes(shape):
    return lax.broadcasted_iota(jnp.int32, shape, 0)


def key_of(first, second):
    low_half = lax.rem(lanes(first.shape), 64) < 32
    return jnp.where(low_half, first, pltpu.roll(second, 32, axis=1))


def value_of(first, second):
    low_half = lax.rem(lanes(first.shape), 64) < 32
    return jnp.where(low_half, pltpu.roll(first, 96, axis=1), second)


def turned(rows, cosine, sine):
    return rows * cosine + pltpu.roll(rows, 64, axis=1) * sine


def backward(
    xp, cot, rq, qp, kvp, qr, kvr, low, rkv, cosine, sine, plen, rlen, flags, ratios,
    ctx, grad, ups,
    flat, rows_s, rows_l, rows_g, us, ul, upf, ups_s, ups_l, gs, gl, send, recv,
):
    me = Place()
    wires = Wires(send, recv)
    count = greet(group_peers(me, "tensor") + group_peers(me, "fsdp"))
    scale = 1.0 / math.sqrt(HD)
    table_c, table_s = cosine[...], sine[...]
    where_q = lax.rem(sublanes((2 * SEQ, SEQ)), SEQ)
    where_k = lanes((2 * SEQ, SEQ))

    def attend(query, keyvalue, lengths, s):
        at = pl.ds(s * SEQ, SEQ)
        key = turned(key_of(keyvalue[0, at, :], keyvalue[1, at, :]), table_c, table_s).astype(BF16)
        value = value_of(keyvalue[0, at, :], keyvalue[1, at, :]).astype(BF16)
        queries = jnp.concatenate(
            [turned(query[at, pl.ds(h * HD, HD)], table_c, table_s) for h in range(2)], axis=0
        ).astype(BF16)
        scores = dot_nt(queries, key) * scale
        allowed = (where_k <= where_q) & (where_k < lengths[s])
        scores = jnp.where(allowed, scores, MASKED)
        top = jnp.max(scores, axis=1, keepdims=True)
        exponent = jnp.exp(scores - top)
        probs = exponent / jnp.sum(exponent, axis=1, keepdims=True)
        return key, value, probs

    signs = [2.0 * flags[i].astype(F32) - 1.0 for i in range(2)]
    margin = 0.1 * (signs[0] * ratios[0] + signs[1] * ratios[1])
    gate = 0.1 / (1.0 + jnp.exp(jnp.full((SEQ, HD), margin, F32)))
    live = sublanes((SEQ, HD))
    raise_v = value_of(rkv[0].astype(F32), rkv[1].astype(F32)).astype(BF16)
    nothing = jnp.zeros((64, HD), BF16)
    rows_v = jnp.concatenate([nothing, raise_v], axis=0)
    rows_q = [jnp.concatenate([rq[:, pl.ds(h * HD, HD)], nothing], axis=0) for h in range(2)]
    up_q = [jnp.zeros((64, HD), F32) for _ in range(2)]
    up_v = jnp.zeros((64, HD), F32)
    for s in range(2):
        at = pl.ds(s * SEQ, SEQ)
        key, value, probs = attend(qp, kvp, plen, s)
        factor = jnp.where(live < plen[s], -signs[s] * gate, 0.0)
        d_context = jnp.concatenate(
            [cot[at, pl.ds(h * HD, HD)].astype(F32) * factor for h in range(2)], axis=0
        ).astype(BF16)
        d_probs = dot_nt(d_context, value)
        delta = jnp.sum(probs * d_probs, axis=1, keepdims=True)
        d_scores = (probs * (d_probs - delta) * scale).astype(BF16)
        d_query = dot(d_scores, key)
        d_value = dot_tn(probs.astype(BF16), d_context)
        high = d_value.astype(BF16)
        rest = (d_value - high.astype(F32)).astype(BF16)
        lows = low[at, :]
        out = dot_nt(high, rows_v) + dot_nt(rest, rows_v)
        for h in range(2):
            turned_back = turned(d_query[h * SEQ : (h + 1) * SEQ], table_c, -table_s).astype(BF16)
            out = out + dot_nt(turned_back, rows_q[h])
            up_q[h] = up_q[h] + dot_tn(lows, turned_back)[:64]
        up_v = up_v + (dot_tn(lows, high) + dot_tn(lows, rest))[64:]
        flat[at, :] = out
    for i in range(NT):
        rows_s[i] = flat[pl.ds(12 * i, 12), :]
    met(count)
    rbase = scatter_start(wires, me, "tensor", rows_s, rows_l)

    us[...] = up_v
    quarter = lax.rem(me.t, 4)
    first = me.t - quarter
    ubase = wires.slots(3)
    for d in range(1, 4):
        wires.copy(us, ul.at[quarter], ubase + d - 1, (me.f, first + lax.rem(quarter + d, 4)))
    ul[quarter] = up_v

    for s in range(2):
        at = pl.ds(s * SEQ, SEQ)
        key, value, probs = attend(qr, kvr, rlen, s)
        context = dot(probs.astype(BF16), value).astype(BF16)
        for h in range(2):
            ctx[at, pl.ds(h * HD, HD)] = context[h * SEQ : (h + 1) * SEQ]

    piece = scatter_sum(wires, me, "tensor", rows_l, rbase)
    rows_g[me.t] = piece
    gbase = gather_start(wires, me, "tensor", rows_g)
    for d in range(1, 4):
        wires.arrived(ul.at[lax.rem(quarter + 4 - d, 4)], ubase + d - 1, (me.f, me.t))
    upf[pl.ds(0, 64), :] = 2.0 * up_q[0]
    upf[pl.ds(64, 64), :] = 2.0 * up_q[1]
    upf[pl.ds(128, 64), :] = 2.0 * (ul[0] + ul[1] + ul[2] + ul[3])
    for i in range(NF):
        ups_s[i] = upf[pl.ds(6 * i, 6), :]
    upbase = scatter_start(wires, me, "fsdp", ups_s, ups_l)
    gather_wait(wires, me, "tensor", rows_g, gbase)
    for i in range(NT):
        flat[pl.ds(12 * i, 12), :] = rows_g[i]
    down = 2.0 * dot_tn(xp[...], flat[...].astype(BF16))
    gs[...] = down.reshape(NF, 16, 128)
    dbase = scatter_start(wires, me, "fsdp", gs, gl)
    ups[me.f] = scatter_sum(wires, me, "fsdp", ups_l, upbase)
    upgather = gather_start(wires, me, "fsdp", ups)
    grad[me.f] = scatter_sum(wires, me, "fsdp", gl, dbase)
    downgather = gather_start(wires, me, "fsdp", grad)
    gather_wait(wires, me, "fsdp", ups, upgather)
    gather_wait(wires, me, "fsdp", grad, downgather)
    wires.drain()


def tables():
    position = np.arange(SEQ, dtype=np.float32)
    inverse = (500000.0 ** (-(np.arange(HD // 2, dtype=np.float32) * 2.0) / HD)).astype(np.float32)
    phase = (position[:, None] * inverse[None, :]).astype(np.float32)
    cosine, sine = np.cos(phase), np.sin(phase)
    return (
        jnp.asarray(np.concatenate([cosine, cosine], axis=1), F32),
        jnp.asarray(np.concatenate([-sine, sine], axis=1), F32),
    )


def shape(dims, dtype):
    return jax.ShapeDtypeStruct(dims, dtype)


def shards(
    policy_token_inputs,
    reference_tokens,
    cotangent,
    query_weight,
    key_weight,
    value_weight,
    query_down,
    value_down,
    query_raise_factor,
    value_raise_factor,
    policy_lengths,
    reference_lengths,
    chosen_flags,
    log_ratios,
):
    cosine, sine = tables()
    kvx = jnp.concatenate(
        [
            jnp.concatenate([key_weight, value_weight], axis=1),
            jnp.concatenate([jnp.zeros_like(value_raise_factor), value_raise_factor], axis=1),
        ],
        axis=0,
    )
    down = jnp.concatenate([query_down, value_down], axis=1)
    qp, kvp, qr, kvr, low, rkv = pl.pallas_call(
        project,
        out_shape=(
            shape((TOK, 256), F32),
            shape((2, TOK, HD), F32),
            shape((TOK, 256), F32),
            shape((2, TOK, HD), F32),
            shape((TOK, HD), BF16),
            shape((2, 64, HD), BF16),
        ),
        in_specs=[VM] * 6,
        out_specs=(VM,) * 6,
        scratch_shapes=[
            pltpu.VMEM((2, 384, 2048), BF16),
            pltpu.VMEM((2, 2048, 256), BF16),
            pltpu.VMEM((2, 2048, 128), BF16),
            pltpu.VMEM((320, 64), BF16),
            pltpu.VMEM((320, 128), BF16),
            pltpu.VMEM((TOK, 128), F32),
            pltpu.VMEM((NT, 12, 128), F32),
            pltpu.VMEM((NT, 12, 128), F32),
            pltpu.VMEM((NT, 12, 128), F32),
            pltpu.VMEM((2, 3, TOK, 256), F32),
            pltpu.VMEM((2, 3, TOK, 256), F32),
            pltpu.VMEM((2, 3, TOK, 256), F32),
            pltpu.VMEM((2, 2, TOK, 256), F32),
            pltpu.SemaphoreType.DMA((160,)),
            pltpu.SemaphoreType.DMA((160,)),
            pltpu.SemaphoreType.DMA((2,)),
        ],
        compiler_params=pltpu.CompilerParams(collective_id=0, has_side_effects=True),
        name="project",
    )(policy_token_inputs, reference_tokens, query_weight, kvx, down, query_raise_factor)
    context, grad, ups = pl.pallas_call(
        backward,
        out_shape=(
            shape((TOK, 256), BF16),
            shape((NF, 16, 128), F32),
            shape((NF, 6, 128), F32),
        ),
        in_specs=[VM] * 11 + [SM] * 4,
        out_specs=(VM,) * 3,
        scratch_shapes=[
            pltpu.VMEM((TOK, 128), F32),
            pltpu.VMEM((NT, 12, 128), F32),
            pltpu.VMEM((NT, 12, 128), F32),
            pltpu.VMEM((NT, 12, 128), F32),
            pltpu.VMEM((64, 128), F32),
            pltpu.VMEM((4, 64, 128), F32),
            pltpu.VMEM((TOK, 128), F32),
            pltpu.VMEM((NF, 6, 128), F32),
            pltpu.VMEM((NF, 6, 128), F32),
            pltpu.VMEM((NF, 16, 128), F32),
            pltpu.VMEM((NF, 16, 128), F32),
            pltpu.SemaphoreType.DMA((170,)),
            pltpu.SemaphoreType.DMA((170,)),
        ],
        compiler_params=pltpu.CompilerParams(collective_id=1, has_side_effects=True),
        name="backward",
    )(
        policy_token_inputs, cotangent, query_raise_factor, qp, kvp, qr, kvr, low, rkv,
        cosine, sine, policy_lengths, reference_lengths, chosen_flags, log_ratios,
    )
    grad = grad.reshape(512, 128)
    ups = ups.reshape(TOK, 128)
    query_up = jnp.concatenate([ups[:64], ups[64:128]], axis=1)
    piece = lax.rem(lax.axis_index("tensor"), 4)
    value_up = lax.dynamic_slice_in_dim(ups[128:], piece * 32, 32, axis=1)
    return context, grad[:, :64], grad[:, 64:], query_up, value_up


def solution(mesh):
    return jax.shard_map(
        shards,
        mesh=mesh,
        in_specs=(
            P("fsdp", "tensor"),
            P("fsdp", "tensor"),
            P("fsdp", "tensor"),
            P("fsdp", "tensor"),
            P("fsdp", "tensor"),
            P("fsdp", "tensor"),
            P("tensor", None),
            P("tensor", None),
            P(None, "tensor"),
            P(None, "tensor"),
            P("fsdp"),
            P("fsdp"),
            P("fsdp"),
            P("fsdp"),
        ),
        out_specs=(
            P("fsdp", "tensor"),
            P("tensor", None),
            P("tensor", None),
            P(None, "tensor"),
            P(None, "tensor"),
        ),
        check_vma=False,
    )
```

time: 405 us -> 138 us (0.34)
  waiting for transfers between devices: 259 us -> 0 us
  Pallas kernels: 0 us -> 128 us
  starting transfers between devices: 47.1 us -> 0 us
  matrix products: 29.6 us -> 0 us
  blocking collectives: 26.4 us -> 0 us
  between operations: 15.5 us -> 0.72 us
  local copies, waits for them, and re-layouts: 15.9 us -> 6.75 us
  other arithmetic: 10 us -> 2.14 us
    all_gather x2 -> x0, waiting for transfers between devices: 171 us -> none  [side_by_side(): lax.all_gather(both, axis, axis=dim, tiled=True)]
    pallas_call x0 -> x2, Pallas kernels: none -> 128 us  [the longest x1 86.8 us: shards(): pl.pallas_call(project, out_shape=(shape((TOK, 256), F32), shape((2, TOK,...]
    all_to_all x3 -> x0, waiting for transfers between devices: 77.9 us -> none  [from_everyone(): return lax.all_to_all(copies, axis, split_axis=0, concat_axis=0, tiled=True)]
    dot_general x21 -> x0, matrix products: 28.9 us -> none  [the longest x6 23.7 us: accumulate(): jnp.dot(tokens, weight_piece, preferred_element_type=jnp.float32)]
    all_to_all x1 -> x0, blocking collectives: 26.4 us -> none  [sent_and_summed(): blocks = lax.all_to_all(cut_along(value, dim, size), axis, 0, 0, tiled=True)]
    ppermute x10 -> x0, starting transfers between devices: 24.9 us -> none  [partner_2(): return lax.ppermute(block, axis, route)]
    all_to_all x3 -> x0, starting transfers between devices: 22.1 us -> none  [from_everyone(): return lax.all_to_all(copies, axis, split_axis=0, concat_axis=0, tiled=True)]
    ppermute x10 -> x0, waiting for transfers between devices: 9.93 us -> none  [partner_2(): return lax.ppermute(block, axis, route)]
  transfers between devices with their start and end apart: 15 -> 0, of which waited for: 9 -> 0; matrix products, arithmetic and copies ran while one was open for 9% -> 0% of each run, Pallas kernels for 0% -> 0%
where the time goes in v1:
time: 138 us
  Pallas kernels  128 us (93%)
  local copies, waits for them, and re-layouts  6.75 us (5%)
  other arithmetic  2.14 us (2%)
    pallas_call x1, Pallas kernels, shards(): pl.pallas_call(project, out_shape=(shape((TOK, 256), F32), shape((2, TOK,...  86.8 us
    pallas_call x1, Pallas kernels, shards(): pl.pallas_call(backward, out_shape=(shape((TOK, 256), BF16), shape((NF, 1...  41.5 us
    unnamed x21, local copies, waits for them, and re-layouts  5.62 us

profile of v1, /device:TPU:1, one launch (start us, length us, event | category | flops | bytes accessed | tf_op | source)
XLA Modules:
  0.0 137.9 jit_solution(1600526725561907816)
XLA Ops:
  0.6 0.0 copy-start.2
  0.6 1.0 copy.32
  1.6 0.0 copy-done.2
  1.6 0.1 copy.33
  1.8 0.0 copy-start.3
  1.8 0.8 pad_maximum_fusion.down
  2.5 0.0 copy-done.3
  2.5 0.0 copy-start.4
  2.6 0.1 copy.29
  2.7 0.6 copy-done.4
  3.3 0.0 copy-start.5
  3.3 0.1 copy.30
  3.4 0.6 copy-done.5
  4.0 0.1 copy.31
  4.1 0.7 fusion.1.kvx
  4.8 86.8 %project.1 = (f32[192,256]{1,0:T(8,128)}, f32[2,192,128]{2,1,0:T(8,128)}, f32[192,256]{1,0:T(8,128)}, f32[2,192,128]{2,1,0:T(8,128)}, bf16[192,128]{1,0:T(8,128)(2,1)}, /*index=5*/bf16[2,64,128]{2,1,0:T(8,128)(2,1)}) custom-call(bf16[192,512]{1,0:T(8,128)(2,1)} %xp.3, bf16[192,512]{1,0:T(8,128)(2,1)} %xr.1, bf16[256,256]{1,0:T(8,128)(2,1)} %wq.1, ...), custom_call_target="tpu_custom_call" | custom-call | tf_op jit(solution)/shard_map/project/pallas_call | solution.py:579
  91.6 41.5 %backward.1 = (bf16[192,256]{1,0:T(8,128)(2,1)}, f32[32,16,128]{2,1,0:T(8,128)}, f32[32,6,128]{2,1,0:T(8,128)}) custom-call(bf16[192,512]{1,0:T(8,128)(2,1)} %xp.3, bf16[192,256]{1,0:T(8,128)(2,1)} %cot.1, bf16[64,256]{1,0:T(8,128)(2,1)} %rq.3, f32[192,256]{1,0:T(8,128)} %get-tuple-element.14.qp, f32[2,192,128]{2,1,0:T(8,128)} %get-tuple-element.15.kvp, ...), custom_call_target="tpu_custom_call" | custom-call | tf_op jit(solution)/shard_map/backward/pallas_call | solution.py:612
  133.1 0.9 reshape.17
  134.0 0.0 copy-start
  134.0 0.6 pad_maximum_fusion.1
  134.7 0.1 constant_dynamic-slice_fusion
  134.8 0.7 copy.36
  135.4 0.0 copy-done
  135.4 0.1 fusion.2
  135.6 0.8 copy.37
  136.4 0.0 copy-start.1
  136.4 0.8 copy.38
  137.1 0.1 copy-done.1
  137.2 0.6 copy.40
  (1 shorter events, 0.0 us)
Async XLA Ops:
  0.6 1.0 copy-start.2
  1.8 0.8 copy-start.3
  2.5 0.7 copy-start.4
  3.3 0.7 copy-start.5
  134.0 1.4 %copy-start = (f32[32,16,128]{2,1,0:T(8,128)S(1)}, f32[32,16,128]{2,1,0:T(8,128)}, u32[]{:S(2)}) copy-start(f32[32,16,128]{2,1,0:T(8,128)} %get-tuple-element.21) | copy-start | bytes 786436
  136.4 0.9 copy-start.1

commit v2 on v1

v2 whole, which is shorter than its diff:
```python
import math

import jax
import jax.numpy as jnp
import numpy as np
from jax import lax
from jax.experimental import pallas as pl
from jax.experimental.pallas import tpu as pltpu
from jax.sharding import PartitionSpec as P

HD = 128
SEQ = 96
TOK = 192
MASKED = -1e30
F32 = jnp.float32
BF16 = jnp.bfloat16
MESH = pl.DeviceIdType.MESH
VM = pl.BlockSpec(memory_space=pltpu.VMEM)
SM = pl.BlockSpec(memory_space=pltpu.SMEM)
NT = 16
NF = 32


def dot(a, b):
    return jnp.dot(a, b, preferred_element_type=F32)


def dot_nt(a, b):
    return lax.dot_general(a, b, (((1,), (1,)), ((), ())), preferred_element_type=F32)


def dot_tn(a, b):
    return lax.dot_general(a, b, (((0,), (0,)), ((), ())), preferred_element_type=F32)


class Place:
    def __init__(self):
        self.f = lax.axis_index("fsdp")
        self.t = lax.axis_index("tensor")
        self.c = lax.rem(self.f, 2)
        self.yh = lax.rem(self.f // 2, 4)
        self.x = self.f // 8
        self.yl = lax.rem(self.t, 2)
        self.z = self.t // 2

    def at(self, x=None, yh=None, c=None, z=None, yl=None):
        x = self.x if x is None else x
        yh = self.yh if yh is None else yh
        c = self.c if c is None else c
        z = self.z if z is None else z
        yl = self.yl if yl is None else yl
        return ((x * 4 + yh) * 2 + c, z * 2 + yl)


class Wires:
    def __init__(self, send, recv):
        self.send, self.recv = send, recv
        self.sent, self.got, self.pending = 0, 0, []

    def slots(self, count):
        base = self.got
        self.got += count
        return base

    def copy(self, src, dst, slot, device, start=True):
        copy = pltpu.make_async_remote_copy(
            src_ref=src,
            dst_ref=dst,
            send_sem=self.send.at[self.sent],
            recv_sem=self.recv.at[slot],
            device_id=device,
            device_id_type=MESH,
        )
        self.sent += 1
        if start:
            copy.start()
            self.pending.append(copy)
        return copy

    def arrived(self, dst, slot, device):
        pltpu.make_async_remote_copy(
            src_ref=dst,
            dst_ref=dst,
            send_sem=self.send.at[0],
            recv_sem=self.recv.at[slot],
            device_id=device,
            device_id_type=MESH,
        ).wait_recv()

    def drain(self):
        for copy in self.pending:
            copy.wait_send()


def greet(devices):
    barrier = pltpu.get_barrier_semaphore()
    for device in devices:
        pl.semaphore_signal(barrier, inc=1, device_id=device, device_id_type=MESH)
    return len(devices)


def met(count):
    pl.semaphore_wait(pltpu.get_barrier_semaphore(), count)


def group_peers(me, axis):
    if axis == "tensor":
        return [(me.f, lax.rem(me.t + d, NT)) for d in range(1, NT)]
    return [(lax.rem(me.f + d, NF), me.t) for d in range(1, NF)]


def scatter_start(wires, me, axis, pieces, landing):
    mine = me.t if axis == "tensor" else me.f
    peers = group_peers(me, axis)
    base = wires.slots(len(peers))
    for d, peer in enumerate(peers):
        to = peer[1] if axis == "tensor" else peer[0]
        wires.copy(pieces.at[to], landing.at[mine], base + d, peer)
    landing[mine] = pieces[mine]
    return base


def scatter_sum(wires, me, axis, landing, base):
    size = NT if axis == "tensor" else NF
    mine = me.t if axis == "tensor" else me.f
    for d in range(1, size):
        source = lax.rem(mine + size - d, size)
        wires.arrived(landing.at[source], base + d - 1, (me.f, me.t))
    total = landing[0].astype(F32)
    for i in range(1, size):
        total = total + landing[i].astype(F32)
    return total


def gather_start(wires, me, axis, blocks):
    mine = me.t if axis == "tensor" else me.f
    peers = group_peers(me, axis)
    base = wires.slots(len(peers))
    for d, peer in enumerate(peers):
        wires.copy(blocks.at[mine], blocks.at[mine], base + d, peer)
    return base


def gather_wait(wires, me, axis, blocks, base):
    size = NT if axis == "tensor" else NF
    mine = me.t if axis == "tensor" else me.f
    for d in range(1, size):
        source = lax.rem(mine + size - d, size)
        wires.arrived(blocks.at[source], base + d - 1, (me.f, me.t))


def lanes(dims):
    return lax.broadcasted_iota(jnp.int32, dims, len(dims) - 1)


def sublanes(dims):
    return lax.broadcasted_iota(jnp.int32, dims, 0)


def turned(rows, cosine, sine):
    return rows * cosine + pltpu.roll(rows, 64, axis=1) * sine


def one_step(
    xp, xr, cot, wq, wkt, wvt, qdt, vdt, rq, rvt, cosine, sine, plen, rlen, flags, ratios,
    ctx, qd_t, vd_t, up_q, up_vt,
    xg, wgq, wgk, kvo, rvx, rvh, low, flat, lows, lowl, lowg,
    kvp, kvs, kvr, kve, kvf, kvz, qpt, qs, qr, qe, query,
    rows_s, rows_l, rows_g, us, ul, upf, ups_s, ups_l, ups, gs, gl, grad, send, recv, local,
):
    me = Place()
    c, z, x, yh, yl = me.c, me.z, me.x, me.yh, me.yl
    wires = Wires(send, recv)
    sibling = me.at(c=1 - c)
    ypair = me.at(yl=1 - yl)
    zpair = me.at(z=z + 1 - 2 * lax.rem(z, 2))
    zs = (me.at(z=lax.rem(z + 1, 8)), me.at(z=lax.rem(z + 7, 8)))
    xs = (me.at(x=lax.rem(x + 1, 4)), me.at(x=lax.rem(x + 3, 4)))
    across = [me.at(yh=lax.rem(yh + d, 4), yl=1 - yl) for d in range(1, 4)]
    count = greet(group_peers(me, "tensor") + group_peers(me, "fsdp") + across)
    quarter = lax.rem(me.t, 4)
    four = me.t - quarter
    quarters = [(me.f, four + lax.rem(quarter + d, 4)) for d in range(1, 4)]

    def rows(o):
        return pl.ds(pl.multiple_of((c if o == 0 else 1 - c) * TOK, TOK), TOK)

    def features(block):
        return pl.ds(pl.multiple_of(block * 256, 256), 256)

    def xblock(kind, o, zz):
        return xg.at[kind, rows(o), features(zz)]

    def half(ref, which):
        return ref.at[:, features(which)]

    inputs = (xp, xr)
    own = []
    for kind in range(2):
        own.append(pltpu.make_async_copy(half(inputs[kind], c), xblock(kind, 0, z), local.at[kind]))
        own[-1].start()

    kvo[pl.ds(0, 32), :] = wkt[...]
    kvo[pl.ds(32, 32), :] = wvt[...]
    rvx[...] = jnp.zeros((128, 64), BF16)
    rvx[pl.ds(pl.multiple_of(yl * 64 + 32, 32), 32), :] = rvt[...]
    my_quarter = pl.ds(pl.multiple_of(quarter * 32, 32), 32)
    rvh[my_quarter, :] = rvt[...]
    down_t = jnp.concatenate([qdt[...], vdt[...]], axis=0)
    flat[...] = dot_nt(xp[...], down_t)
    for i in range(NT):
        lows[i] = flat[pl.ds(12 * i, 12), :]
    met(count)

    yl_d = lax.rem(yh, 2)
    m_own = yh // 2

    def wslot(which, v, xx, m):
        block = features(2 * xx + m)
        if which == 0:
            return wgk.at[pl.ds(pl.multiple_of(v * 64, 64), 64), block]
        return wgq.at[v, block]

    maybe = []

    def y_sends(which, src, base):
        dst = wslot(which, yl, x, m_own)
        slot = base + m_own * 2 + yl
        near = wires.copy(src, dst, slot, me.at(yl=yl_d), start=False)
        maybe.append(near)

        @pl.when(yl == yl_d)
        def _():
            pltpu.make_async_copy(src, dst, recv.at[slot]).start()

        @pl.when(yl != yl_d)
        def _():
            near.start()

        for d in (1, 3, 2):
            wires.copy(src, dst, slot, me.at(yh=lax.rem(yh + d, 4), yl=yl_d))

    ybases = (wires.slots(4), wires.slots(4))
    y_sends(0, kvo, ybases[0])
    sib = wires.slots(2)

    def sib_send(kind):
        wires.copy(half(inputs[kind], 1 - c), xblock(kind, 0, z), sib + kind, sibling)

    zbase = wires.slots(2 * 2 * 2 * 4)

    def zidx(kind, o, way, s):
        return zbase + ((kind * 2 + o) * 2 + way) * 4 + s - 1

    def zblock(way, s):
        return lax.rem(z + (8 - s if way == 0 else s), 8)

    def zlast(o, way):
        return 4 if o == way else 3

    def zsend(kind, o, way, s):
        if s > zlast(o, way):
            return
        block = zblock(way, s - 1)
        src = half(inputs[kind], c) if (s == 1 and o == 0) else xblock(kind, o, block)
        wires.copy(src, xblock(kind, o, block), zidx(kind, o, way, s), zs[way])

    def zstep(kind, s):
        for o in range(2):
            for way in range(2):
                if s <= zlast(o, way):
                    wires.arrived(xblock(kind, o, zblock(way, s)), zidx(kind, o, way, s), zs[way])
                    zsend(kind, o, way, s + 1)

    def zfirst(kind, o):
        if o == 1:
            wires.arrived(xblock(kind, 1, z), sib + kind, sibling)
        zsend(kind, o, 0, 1)
        zsend(kind, o, 1, 1)

    sib_send(0)
    zfirst(0, 0)
    y_sends(1, wq, ybases[1])
    lbase = scatter_start(wires, me, "tensor", lows, lowl)
    vbase = wires.slots(3)
    for d, peer in enumerate(quarters):
        wires.copy(rvt, rvh.at[my_quarter], vbase + d, peer)
    sib_send(1)
    zfirst(0, 1)

    xbase = wires.slots(2 * 4 * 2 * 2)
    orders = (
        [(m_own, yl), (m_own, 1 - yl), (1 - m_own, yl), (1 - m_own, 1 - yl)],
        [(m_own, 1 - yl), (1 - m_own, 1 - yl), (m_own, yl), (1 - m_own, yl)],
    )

    def xidx(which, j, way, s):
        return xbase + ((which * 4 + j) * 2 + way) * 2 + s - 1

    def xfrom(way, s):
        return lax.rem(x + (4 - s if way == 0 else s), 4)

    def ystep(which, j):
        m, v = orders[which][j]
        block = wslot(which, v, x, m)
        wires.arrived(block, ybases[which] + m * 2 + v, ypair)
        for way in range(2):
            wires.copy(block, block, xidx(which, j, way, 1), xs[way])

    def xwait(which, j, way, s):
        m, v = orders[which][j]
        block = wslot(which, v, xfrom(way, s), m)
        wires.arrived(block, xidx(which, j, way, s), xs[way])
        return block

    def xstep(which, j):
        for way in range(2):
            block = xwait(which, j, way, 1)
            if way == j % 2:
                wires.copy(block, block, xidx(which, j, way, 2), xs[way])

    def xend(which, j):
        xwait(which, j, j % 2, 2)

    kbase, qbase = wires.slots(6), wires.slots(6)

    def kv_partial(kind):
        tokens = xg.at[kind]
        kvs[kind] = dot_nt(tokens[rows(1), :], wgk[...])
        wires.copy(kvs.at[kind], kvr.at[kind], kbase + kind * 3, sibling)
        kvp[kind] = dot_nt(tokens[rows(0), :], wgk[...])

    def kv_across(kind):
        wires.arrived(kvr.at[kind], kbase + kind * 3, sibling)
        total = kvp[kind] + kvr[kind]
        if kind == 0:
            total = total + 2.0 * dot_nt(low[:, pl.ds(64, 64)], rvx[...])
        kvp[kind] = total
        wires.copy(kvp.at[kind], kve.at[kind], kbase + kind * 3 + 1, ypair)

    def kv_pieces(kind):
        wires.arrived(kve.at[kind], kbase + kind * 3 + 1, ypair)
        kvf[kind] = kvp[kind] + kve[kind]
        wires.copy(kvf.at[kind], kvz.at[kind], kbase + kind * 3 + 2, zpair)

    def q_partial(kind, g):
        tokens = xg.at[kind]
        weight = wgq.at[1 - yl if g == 0 else yl]
        qs[kind, g] = dot(tokens[rows(1), :], weight[...])
        wires.copy(qs.at[kind, g], qr.at[kind, g], qbase + kind * 3 + g, sibling)
        qpt[kind, g] = dot(tokens[rows(0), :], weight[...])

    def q_across(kind):
        wires.arrived(qr.at[kind, 0], qbase + kind * 3, sibling)
        qpt[kind, 0] = qpt[kind, 0] + qr[kind, 0]
        wires.copy(qpt.at[kind, 0], qe.at[kind], qbase + kind * 3 + 2, ypair)

    def q_final(kind):
        wires.arrived(qr.at[kind, 1], qbase + kind * 3 + 1, sibling)
        wires.arrived(qe.at[kind], qbase + kind * 3 + 2, ypair)
        total = qpt[kind, 1] + qr[kind, 1] + qe[kind]
        if kind == 0:
            total = total + 2.0 * dot(low[:, pl.ds(0, 64)], rq[...])
        query[kind] = total

    scale = 1.0 / math.sqrt(HD)
    table_c, table_s = cosine[...], sine[...]
    where_q = lax.rem(sublanes((2 * SEQ, SEQ)), SEQ)
    where_k = lanes((2 * SEQ, SEQ))
    group = lanes((SEQ, HD)) // 32
    even = lax.rem(z, 2) == 0

    def heads_of(kind, s):
        at = pl.ds(s * SEQ, SEQ)
        mine, theirs = kvf[kind, at, :], kvz[kind, at, :]
        a, b = jnp.where(even, mine, theirs), jnp.where(even, theirs, mine)
        a96, b32 = pltpu.roll(a, 96, axis=1), pltpu.roll(b, 32, axis=1)
        key = jnp.where(group == 0, a, jnp.where(group == 1, a96, jnp.where(group == 2, pltpu.roll(b, 64, axis=1), b32)))
        value = jnp.where(group == 0, a96, jnp.where(group == 1, pltpu.roll(a, 64, axis=1), jnp.where(group == 2, b32, b)))
        return turned(key, table_c, table_s).astype(BF16), value.astype(BF16)

    def attend(kind, key, lengths, s):
        at = pl.ds(s * SEQ, SEQ)
        queries = jnp.concatenate(
            [turned(query[kind, at, pl.ds(h * HD, HD)], table_c, table_s) for h in range(2)], axis=0
        ).astype(BF16)
        scores = dot_nt(queries, key) * scale
        allowed = (where_k <= where_q) & (where_k < lengths[s])
        scores = jnp.where(allowed, scores, MASKED)
        top = jnp.max(scores, axis=1, keepdims=True)
        exponent = jnp.exp(scores - top)
        return exponent / jnp.sum(exponent, axis=1, keepdims=True)

    ystep(0, 0)
    ystep(0, 1)
    ystep(1, 0)
    zstep(0, 1)
    xstep(0, 0)
    xstep(0, 1)
    ystep(0, 2)
    ystep(0, 3)
    ystep(1, 1)
    xstep(0, 2)
    xstep(0, 3)
    zstep(0, 2)
    ystep(1, 2)
    xstep(1, 0)
    piece = scatter_sum(wires, me, "tensor", lowl, lbase)
    lowg[me.t] = piece
    gbase = gather_start(wires, me, "tensor", lowg)
    xstep(1, 1)
    ystep(1, 3)
    zstep(0, 3)
    zfirst(1, 0)
    zfirst(1, 1)
    xstep(1, 2)
    gather_wait(wires, me, "tensor", lowg, gbase)
    for i in range(NT):
        flat[pl.ds(12 * i, 12), :] = lowg[i]
    low[...] = flat[...].astype(BF16)
    zstep(0, 4)
    for copy in own:
        copy.wait()
    for j in range(4):
        xend(0, j)
    kv_partial(0)
    xstep(1, 3)
    zstep(1, 1)
    kv_across(0)
    xend(1, 0)
    xend(1, 1)
    q_partial(0, 0)
    zstep(1, 2)
    kv_pieces(0)
    q_across(0)
    zstep(1, 3)
    xend(1, 2)
    xend(1, 3)
    q_partial(0, 1)
    zstep(1, 4)
    wires.arrived(kvz.at[0], kbase + 2, zpair)
    pair = [heads_of(0, s) for s in range(2)]
    for d in range(1, 4):
        theirs = pl.ds(pl.multiple_of(lax.rem(quarter + 4 - d, 4) * 32, 32), 32)
        wires.arrived(rvh.at[theirs], vbase + d - 1, ypair)
    q_final(0)

    signs = [2.0 * flags[i].astype(F32) - 1.0 for i in range(2)]
    margin = 0.1 * (signs[0] * ratios[0] + signs[1] * ratios[1])
    gate = 0.1 / (1.0 + jnp.exp(jnp.full((SEQ, HD), margin, F32)))
    live = sublanes((SEQ, HD))
    rows_v = jnp.concatenate([jnp.zeros((128, 64), BF16), rvh[...]], axis=1)
    nothing = jnp.zeros((64, HD), BF16)
    rows_q = [jnp.concatenate([rq[:, pl.ds(h * HD, HD)], nothing], axis=0) for h in range(2)]
    grads_q = [[], []]
    grads_v = []
    for s in range(2):
        at = pl.ds(s * SEQ, SEQ)
        key, value = pair[s]
        probs = attend(0, key, plen, s)
        factor = jnp.where(live < plen[s], -signs[s] * gate, 0.0)
        d_context = jnp.concatenate(
            [cot[at, pl.ds(h * HD, HD)].astype(F32) * factor for h in range(2)], axis=0
        ).astype(BF16)
        d_probs = dot_nt(d_context, value)
        delta = jnp.sum(probs * d_probs, axis=1, keepdims=True)
        d_scores = (probs * (d_probs - delta) * scale).astype(BF16)
        d_query = dot(d_scores, key)
        d_value = dot_tn(probs.astype(BF16), d_context)
        high = d_value.astype(BF16)
        rest = (d_value - high.astype(F32)).astype(BF16)
        out = dot(high, rows_v) + dot(rest, rows_v)
        for h in range(2):
            turned_back = turned(d_query[h * SEQ : (h + 1) * SEQ], table_c, -table_s).astype(BF16)
            out = out + dot_nt(turned_back, rows_q[h])
            grads_q[h].append(turned_back)
        grads_v.append((high, rest))
        flat[at, :] = out
    for i in range(NT):
        rows_s[i] = flat[pl.ds(12 * i, 12), :]
    rbase = scatter_start(wires, me, "tensor", rows_s, rows_l)

    lows2 = [low[pl.ds(s * SEQ, SEQ), :] for s in range(2)]
    total_v = sum(dot_tn(part, lows2[s]) for s in range(2) for part in grads_v[s])
    for q in range(4):
        us[q] = 2.0 * total_v[q * 32 : (q + 1) * 32]
    ubase = wires.slots(3)
    for d, peer in enumerate(quarters):
        wires.copy(us.at[lax.rem(quarter + d + 1, 4)], ul.at[quarter], ubase + d, peer)
    ul[quarter] = us[quarter]
    for h in range(2):
        total_q = sum(dot_tn(lows2[s], grads_q[h][s]) for s in range(2))
        upf[pl.ds(h * 64, 64), :] = 2.0 * total_q[:64]

    kv_partial(1)
    q_partial(1, 0)
    rows_g[me.t] = scatter_sum(wires, me, "tensor", rows_l, rbase)
    gbase = gather_start(wires, me, "tensor", rows_g)
    kv_across(1)
    q_across(1)
    q_partial(1, 1)
    for d in range(1, 4):
        wires.arrived(ul.at[lax.rem(quarter + 4 - d, 4)], ubase + d - 1, ypair)
    upf[pl.ds(128, 32), :] = ul[0] + ul[1] + ul[2] + ul[3]
    for i in range(NF):
        ups_s[i] = upf[pl.ds(5 * i, 5), :]
    upbase = scatter_start(wires, me, "fsdp", ups_s, ups_l)
    gather_wait(wires, me, "tensor", rows_g, gbase)
    for i in range(NT):
        flat[pl.ds(12 * i, 12), :] = rows_g[i]
    down = 2.0 * dot_tn(flat[...].astype(BF16), xp[...])
    for i in range(8):
        for j in range(4):
            gs[i * 4 + j] = down[i * 16 : (i + 1) * 16, j * 128 : (j + 1) * 128].astype(BF16)
    dbase = scatter_start(wires, me, "fsdp", gs, gl)
    kv_pieces(1)
    q_final(1)
    ups[me.f] = scatter_sum(wires, me, "fsdp", ups_l, upbase)
    upgather = gather_start(wires, me, "fsdp", ups)
    grad[me.f] = scatter_sum(wires, me, "fsdp", gl, dbase).astype(BF16)
    downgather = gather_start(wires, me, "fsdp", grad)

    wires.arrived(kvz.at[1], kbase + 5, zpair)
    for s in range(2):
        at = pl.ds(s * SEQ, SEQ)
        key, value = heads_of(1, s)
        context = dot(attend(1, key, rlen, s).astype(BF16), value).astype(BF16)
        for h in range(2):
            ctx[at, pl.ds(h * HD, HD)] = context[h * SEQ : (h + 1) * SEQ]

    gather_wait(wires, me, "fsdp", ups, upgather)
    for i in range(NF):
        upf[pl.ds(5 * i, 5), :] = ups[i]
    for h in range(2):
        up_q[:, pl.ds(h * 128, 128)] = upf[pl.ds(h * 64, 64), :]
    up_vt[...] = upf[pl.ds(128, 32), pl.ds(64, 64)]
    gather_wait(wires, me, "fsdp", grad, downgather)
    for i in range(8):
        target = qd_t if i < 4 else vd_t
        for j in range(4):
            target[pl.ds((i % 4) * 16, 16), pl.ds(j * 128, 128)] = grad[i * 4 + j].astype(F32)
    for near in maybe:

        @pl.when(yl != yl_d)
        def _(near=near):
            near.wait_send()

    wires.drain()


def tables():
    position = np.arange(SEQ, dtype=np.float32)
    inverse = (500000.0 ** (-(np.arange(HD // 2, dtype=np.float32) * 2.0) / HD)).astype(np.float32)
    phase = (position[:, None] * inverse[None, :]).astype(np.float32)
    cosine, sine = np.cos(phase), np.sin(phase)
    return (
        jnp.asarray(np.concatenate([cosine, cosine], axis=1), F32),
        jnp.asarray(np.concatenate([-sine, sine], axis=1), F32),
    )


def shape(dims, dtype):
    return jax.ShapeDtypeStruct(dims, dtype)


def shards(
    policy_token_inputs,
    reference_tokens,
    cotangent,
    query_weight,
    key_weight,
    value_weight,
    query_down,
    value_down,
    query_raise_factor,
    value_raise_factor,
    policy_lengths,
    reference_lengths,
    chosen_flags,
    log_ratios,
):
    cosine, sine = tables()
    vm = pltpu.VMEM
    context, qd_t, vd_t, query_up, up_vt = pl.pallas_call(
        one_step,
        out_shape=(
            shape((TOK, 256), BF16),
            shape((64, 512), F32),
            shape((64, 512), F32),
            shape((64, 256), F32),
            shape((32, 64), F32),
        ),
        in_specs=[VM] * 12 + [SM] * 4,
        out_specs=(VM,) * 5,
        scratch_shapes=[
            vm((2, 384, 2048), BF16),
            vm((2, 2048, 256), BF16),
            vm((128, 2048), BF16),
            vm((64, 256), BF16),
            vm((128, 64), BF16),
            vm((128, 64), BF16),
            vm((TOK, 128), BF16),
            vm((TOK, 128), F32),
            vm((NT, 12, 128), F32),
            vm((NT, 12, 128), F32),
            vm((NT, 12, 128), F32),
            *[vm((2, TOK, 128), F32)] * 6,
            *[vm((2, 2, TOK, 256), F32)] * 3,
            *[vm((2, TOK, 256), F32)] * 2,
            *[vm((NT, 12, 128), F32)] * 3,
            *[vm((4, 32, 128), F32)] * 2,
            vm((160, 128), F32),
            *[vm((NF, 5, 128), F32)] * 3,
            *[vm((NF, 16, 128), BF16)] * 3,
            pltpu.SemaphoreType.DMA((300,)),
            pltpu.SemaphoreType.DMA((300,)),
            pltpu.SemaphoreType.DMA((2,)),
        ],
        compiler_params=pltpu.CompilerParams(collective_id=0, has_side_effects=True),
        name="one_step",
    )(
        policy_token_inputs, reference_tokens, cotangent, query_weight, key_weight.T, value_weight.T,
        query_down.T, value_down.T, query_raise_factor, value_raise_factor.T, cosine, sine,
        policy_lengths, reference_lengths, chosen_flags, log_ratios,
    )
    return context, qd_t.T, vd_t.T, query_up, up_vt.T


def solution(mesh):
    return jax.shard_map(
        shards,
        mesh=mesh,
        in_specs=(
            P("fsdp", "tensor"),
            P("fsdp", "tensor"),
            P("fsdp", "tensor"),
            P("fsdp", "tensor"),
            P("fsdp", "tensor"),
            P("fsdp", "tensor"),
            P("tensor", None),
            P("tensor", None),
            P(None, "tensor"),
            P(None, "tensor"),
            P("fsdp"),
            P("fsdp"),
            P("fsdp"),
            P("fsdp"),
        ),
        out_specs=(
            P("fsdp", "tensor"),
            P("tensor", None),
            P("tensor", None),
            P(None, "tensor"),
            P(None, "tensor"),
        ),
        check_vma=False,
    )
```

time: 138 us -> 104 us (0.75)
  Pallas kernels: 128 us -> 98.5 us
  other arithmetic: 2.14 us -> 0 us
  local copies, waits for them, and re-layouts: 6.75 us -> 4.71 us
    pallas_call x2 -> x1, Pallas kernels: 128 us -> 98.5 us  [shards(): pl.pallas_call(one_step, out_shape=(shape((TOK, 256), BF16), shape((64, 5...]
    concatenate x3 -> x0, other arithmetic: 2.14 us -> none  [the longest x1 0.77 us: shards(): down = jnp.concatenate([query_down, value_down], axis=1)]
    unnamed x21 -> x13, local copies, waits for them, and re-layouts: 5.62 us -> 4.71 us
where the time goes in v2:
time: 104 us
  Pallas kernels  98.5 us (95%)
  local copies, waits for them, and re-layouts  4.71 us (5%)
    pallas_call x1, Pallas kernels, shards(): pl.pallas_call(one_step, out_shape=(shape((TOK, 256), BF16), shape((64, 5...  98.5 us
    unnamed x13, local copies, waits for them, and re-layouts  4.71 us

profile of v2, /device:TPU:1, one launch (start us, length us, event | category | flops | bytes accessed | tf_op | source)
XLA Modules:
  0.0 103.9 jit_solution(14034931629759156936)
XLA Ops:
  0.6 98.5 %one_step.1 = (bf16[192,256]{1,0:T(8,128)(2,1)}, f32[64,512]{1,0:T(8,128)}, f32[64,512]{1,0:T(8,128)}, f32[64,256]{1,0:T(8,128)}, f32[32,64]{1,0:T(8,128)}) custom-call(bf16[192,512]{1,0:T(8,128)(2,1)} %xp.1, bf16[192,512]{1,0:T(8,128)(2,1)} %xr.1, bf16[192,256]{1,0:T(8,128)(2,1)} %cot.1, bf16[256,256]{1,0:T(8,128)(2,1)} %wq.1, bf16[32,256]{1,0:T(8,128)(2,1)} %bitcast.12, ...), custom_call_target="tpu_custom_call" | custom-call | tf_op jit(solution)/shard_map/one_step/pallas_call | solution.py:584
  99.2 0.0 copy-start.1
  99.2 1.6 %copy.26 = bf16[192,256]{1,0:T(8,128)(2,1)} copy(bf16[192,256]{1,0:T(8,128)(2,1)} %get-tuple-element.20) | data formatting | bytes 196608
  100.7 0.0 copy-done.1
  100.7 0.0 copy-start
  100.7 0.7 copy.27
  101.4 0.3 copy-done
  101.7 0.0 copy-start.2
  101.7 0.7 copy.28
  102.4 0.2 copy-done.2
  102.6 0.0 copy-start.3
  102.6 0.6 copy.29
  103.2 0.1 copy-done.3
  103.3 0.6 copy.30
Async XLA Ops:
  99.2 1.6 %copy-start.1 = (f32[64,512]{1,0:T(8,128)S(1)}, f32[64,512]{1,0:T(8,128)}, u32[]{:S(2)}) copy-start(f32[64,512]{1,0:T(8,128)} %get-tuple-element.11) | copy-start | bytes 393220
  100.7 1.0 copy-start
  101.7 0.9 copy-start.2
  102.6 0.7 copy-start.3

commit v3 on v2

--- a/solution.py
+++ b/solution.py
@@ -57,39 +57,41 @@
         self.send, self.recv = send, recv
         self.sent, self.got, self.pending = 0, 0, []
 
-    def slots(self, count):
+    def slots(self, count=1):
         base = self.got
         self.got += count
         return base
 
-    def copy(self, src, dst, slot, device, start=True):
-        copy = pltpu.make_async_remote_copy(
+    def sender(self, everything=None):
+        slot = self.sent
+        self.sent += 1
+        if everything is not None:
+            self.pending.append((everything, slot))
+        return slot
+
+    def make(self, src, dst, sender, slot, device):
+        return pltpu.make_async_remote_copy(
             src_ref=src,
             dst_ref=dst,
-            send_sem=self.send.at[self.sent],
+            send_sem=self.send.at[sender],
             recv_sem=self.recv.at[slot],
             device_id=device,
             device_id_type=MESH,
         )
-        self.sent += 1
-        if start:
-            copy.start()
-            self.pending.append(copy)
-        return copy
-
-    def arrived(self, dst, slot, device):
-        pltpu.make_async_remote_copy(
-            src_ref=dst,
-            dst_ref=dst,
-            send_sem=self.send.at[0],
-            recv_sem=self.recv.at[slot],
-            device_id=device,
-            device_id_type=MESH,
-        ).wait_recv()
+
+    def copy(self, src, dst, slot, device, sender=None):
+        sender = self.sender(src) if sender is None else sender
+        self.make(src, dst, sender, slot, device).start()
+
+    def arrived(self, dst, slot):
+        self.make(dst, dst, 0, slot, self.anyone).wait_recv()
+
+    def left(self, src, sender):
+        self.make(src, src, sender, 0, self.anyone).wait_send()
 
     def drain(self):
-        for copy in self.pending:
-            copy.wait_send()
+        for src, sender in self.pending:
+            self.left(src, sender)
 
 
 def greet(devices):
@@ -112,20 +114,17 @@
 def scatter_start(wires, me, axis, pieces, landing):
     mine = me.t if axis == "tensor" else me.f
     peers = group_peers(me, axis)
-    base = wires.slots(len(peers))
-    for d, peer in enumerate(peers):
+    slot, sender = wires.slots(), wires.sender(pieces.at[pl.ds(0, len(peers))])
+    for peer in peers:
         to = peer[1] if axis == "tensor" else peer[0]
-        wires.copy(pieces.at[to], landing.at[mine], base + d, peer)
+        wires.copy(pieces.at[to], landing.at[mine], slot, peer, sender)
     landing[mine] = pieces[mine]
-    return base
-
-
-def scatter_sum(wires, me, axis, landing, base):
+    return slot
+
+
+def scatter_sum(wires, axis, landing, slot):
     size = NT if axis == "tensor" else NF
-    mine = me.t if axis == "tensor" else me.f
-    for d in range(1, size):
-        source = lax.rem(mine + size - d, size)
-        wires.arrived(landing.at[source], base + d - 1, (me.f, me.t))
+    wires.arrived(landing.at[pl.ds(0, size - 1)], slot)
     total = landing[0].astype(F32)
     for i in range(1, size):
         total = total + landing[i].astype(F32)
@@ -135,18 +134,15 @@
 def gather_start(wires, me, axis, blocks):
     mine = me.t if axis == "tensor" else me.f
     peers = group_peers(me, axis)
-    base = wires.slots(len(peers))
-    for d, peer in enumerate(peers):
-        wires.copy(blocks.at[mine], blocks.at[mine], base + d, peer)
-    return base
-
-
-def gather_wait(wires, me, axis, blocks, base):
+    slot, sender = wires.slots(), wires.sender(blocks.at[pl.ds(0, len(peers))])
+    for peer in peers:
+        wires.copy(blocks.at[mine], blocks.at[mine], slot, peer, sender)
+    return slot
+
+
+def gather_wait(wires, axis, blocks, slot):
     size = NT if axis == "tensor" else NF
-    mine = me.t if axis == "tensor" else me.f
-    for d in range(1, size):
-        source = lax.rem(mine + size - d, size)
-        wires.arrived(blocks.at[source], base + d - 1, (me.f, me.t))
+    wires.arrived(blocks.at[pl.ds(0, size - 1)], slot)
 
 
 def lanes(dims):
@@ -171,6 +167,7 @@
     me = Place()
     c, z, x, yh, yl = me.c, me.z, me.x, me.yh, me.yl
     wires = Wires(send, recv)
+    wires.anyone = (me.f, me.t)
     sibling = me.at(c=1 - c)
     ypair = me.at(yl=1 - yl)
     zpair = me.at(z=z + 1 - 2 * lax.rem(z, 2))
@@ -212,8 +209,16 @@
         lows[i] = flat[pl.ds(12 * i, 12), :]
     met(count)
 
-    yl_d = lax.rem(yh, 2)
     m_own = yh // 2
+    is_inner = 1 - lax.rem(yh + yl, 2)
+    inner = is_inner == 1
+
+    def pick(inside, between):
+        return is_inner * inside + (1 - is_inner) * between
+
+    up, below = lax.rem(yh + 1, 4), lax.rem(yh + 3, 4)
+    partner = me.at(yh=lax.rem(yh + 3 + 2 * lax.rem(yh, 2), 4))
+    m_first = pick(m_own, below // 2)
 
     def wslot(which, v, xx, m):
         block = features(2 * xx + m)
@@ -221,33 +226,77 @@
             return wgk.at[pl.ds(pl.multiple_of(v * 64, 64), 64), block]
         return wgq.at[v, block]
 
-    maybe = []
-
-    def y_sends(which, src, base):
+    def part_of(which, v, xx, m, part):
+        block = 2 * xx + m
+        if which == 0:
+            return wgk.at[pl.ds(pl.multiple_of(v * 64 + part * 32, 32), 32), features(block)]
+        return wgq.at[v, pl.ds(pl.multiple_of(block * 256 + part * 128, 128), 128)]
+
+    ybases = (wires.slots(4), wires.slots(4))
+    passed = []
+
+    def y_sends(which, src):
         dst = wslot(which, yl, x, m_own)
-        slot = base + m_own * 2 + yl
-        near = wires.copy(src, dst, slot, me.at(yl=yl_d), start=False)
-        maybe.append(near)
-
-        @pl.when(yl == yl_d)
+        near, base = ybases[which], ybases[which] + 2
+
+        stay = pltpu.make_async_copy(src, dst, local.at[2 + which])
+
+        @pl.when(inner)
         def _():
-            pltpu.make_async_copy(src, dst, recv.at[slot]).start()
-
-        @pl.when(yl != yl_d)
-        def _():
-            near.start()
-
-        for d in (1, 3, 2):
-            wires.copy(src, dst, slot, me.at(yh=lax.rem(yh + d, 4), yl=yl_d))
-
-    ybases = (wires.slots(4), wires.slots(4))
-    y_sends(0, kvo, ybases[0])
+            stay.start()
+
+        to_up = me.at(yh=pick(up, 2 * m_own + 1), yl=pick(yl, 1 - yl))
+        to_below = me.at(yh=pick(below, 2 * m_own), yl=pick(yl, 1 - yl))
+        wires.copy(src, dst, pick(base, near), to_up)
+        wires.copy(src, dst, pick(base + 1, near), to_below)
+
+    def pass_on(which, m, part):
+        piece = part_of(which, yl, x, m, part)
+        to = me.at(yh=up if part == 0 else below)
+        copy = wires.make(piece, piece, wires.sender(), ybases[which] + 2 + part, to)
+        passed.append(copy)
+        return copy
+
+    def y_arrival(which, j):
+        m, v = orders[which][j]
+        block = wslot(which, v, x, m)
+        base = ybases[which]
+        if v is yl:
+            first = m is m_first
+            if first:
+                here = [pltpu.make_async_copy(block, block, local.at[2 + which]).wait]
+            else:
+                parts = [part_of(which, v, x, m, part) for part in range(2)]
+                here = [wires.make(p, p, 0, base + 2 + i, wires.anyone).wait_recv for i, p in enumerate(parts)]
+            whole = wires.make(block, block, 0, base + (2 if first else 3), wires.anyone)
+            onward = pass_on(which, m, 0 if first else 1)
+
+            @pl.when(inner)
+            def _():
+                for wait in here:
+                    wait()
+
+            @pl.when(jnp.logical_not(inner))
+            def _():
+                whole.wait_recv()
+                onward.start()
+
+        elif m is m_own:
+            wires.arrived(block, base)
+            wires.copy(block, block, base + 1, partner)
+        else:
+            wires.arrived(block, base + 1)
+        return block
+
+    y_sends(0, kvo)
     sib = wires.slots(2)
 
     def sib_send(kind):
         wires.copy(half(inputs[kind], 1 - c), xblock(kind, 0, z), sib + kind, sibling)
 
     zbase = wires.slots(2 * 2 * 2 * 4)
+
+    zsender = wires.sender(xg.at[:, :, pl.ds(0, 7 * 256)])
 
     def zidx(kind, o, way, s):
         return zbase + ((kind * 2 + o) * 2 + way) * 4 + s - 1
@@ -263,35 +312,38 @@
             return
         block = zblock(way, s - 1)
         src = half(inputs[kind], c) if (s == 1 and o == 0) else xblock(kind, o, block)
-        wires.copy(src, xblock(kind, o, block), zidx(kind, o, way, s), zs[way])
+        wires.copy(src, xblock(kind, o, block), zidx(kind, o, way, s), zs[way], zsender)
 
     def zstep(kind, s):
         for o in range(2):
             for way in range(2):
                 if s <= zlast(o, way):
-                    wires.arrived(xblock(kind, o, zblock(way, s)), zidx(kind, o, way, s), zs[way])
+                    wires.arrived(xblock(kind, o, zblock(way, s)), zidx(kind, o, way, s))
                     zsend(kind, o, way, s + 1)
 
     def zfirst(kind, o):
         if o == 1:
-            wires.arrived(xblock(kind, 1, z), sib + kind, sibling)
+            wires.arrived(xblock(kind, 1, z), sib + kind)
         zsend(kind, o, 0, 1)
         zsend(kind, o, 1, 1)
 
     sib_send(0)
     zfirst(0, 0)
-    y_sends(1, wq, ybases[1])
-    lbase = scatter_start(wires, me, "tensor", lows, lowl)
-    vbase = wires.slots(3)
-    for d, peer in enumerate(quarters):
-        wires.copy(rvt, rvh.at[my_quarter], vbase + d, peer)
+    y_sends(1, wq)
+    lslot = scatter_start(wires, me, "tensor", lows, lowl)
+    vslot, vsender = wires.slots(), wires.sender(rvh.at[pl.ds(0, 96)])
+    for peer in quarters:
+        wires.copy(rvt, rvh.at[my_quarter], vslot, peer, vsender)
     sib_send(1)
     zfirst(0, 1)
 
     xbase = wires.slots(2 * 4 * 2 * 2)
+    xsenders = [wires.sender(ref) for ref in (wgk.at[:, pl.ds(0, 1536)], wgq.at[:, pl.ds(0, 1536)])]
+    yo = 1 - yl
+    m_other, m_last = 1 - m_own, 1 - m_first
     orders = (
-        [(m_own, yl), (m_own, 1 - yl), (1 - m_own, yl), (1 - m_own, 1 - yl)],
-        [(m_own, 1 - yl), (1 - m_own, 1 - yl), (m_own, yl), (1 - m_own, yl)],
+        [(m_own, yo), (m_first, yl), (m_other, yo), (m_last, yl)],
+        [(m_own, yo), (m_other, yo), (m_first, yl), (m_last, yl)],
     )
 
     def xidx(which, j, way, s):
@@ -301,23 +353,21 @@
         return lax.rem(x + (4 - s if way == 0 else s), 4)
 
     def ystep(which, j):
-        m, v = orders[which][j]
-        block = wslot(which, v, x, m)
-        wires.arrived(block, ybases[which] + m * 2 + v, ypair)
+        block = y_arrival(which, j)
         for way in range(2):
-            wires.copy(block, block, xidx(which, j, way, 1), xs[way])
+            wires.copy(block, block, xidx(which, j, way, 1), xs[way], xsenders[which])
 
     def xwait(which, j, way, s):
         m, v = orders[which][j]
         block = wslot(which, v, xfrom(way, s), m)
-        wires.arrived(block, xidx(which, j, way, s), xs[way])
+        wires.arrived(block, xidx(which, j, way, s))
         return block
 
     def xstep(which, j):
         for way in range(2):
             block = xwait(which, j, way, 1)
             if way == j % 2:
-                wires.copy(block, block, xidx(which, j, way, 2), xs[way])
+                wires.copy(block, block, xidx(which, j, way, 2), xs[way], xsenders[which])
 
     def xend(which, j):
         xwait(which, j, j % 2, 2)
@@ -331,7 +381,7 @@
         kvp[kind] = dot_nt(tokens[rows(0), :], wgk[...])
 
     def kv_across(kind):
-        wires.arrived(kvr.at[kind], kbase + kind * 3, sibling)
+        wires.arrived(kvr.at[kind], kbase + kind * 3)
         total = kvp[kind] + kvr[kind]
         if kind == 0:
             total = total + 2.0 * dot_nt(low[:, pl.ds(64, 64)], rvx[...])
@@ -339,7 +389,7 @@
         wires.copy(kvp.at[kind], kve.at[kind], kbase + kind * 3 + 1, ypair)
 
     def kv_pieces(kind):
-        wires.arrived(kve.at[kind], kbase + kind * 3 + 1, ypair)
+        wires.arrived(kve.at[kind], kbase + kind * 3 + 1)
         kvf[kind] = kvp[kind] + kve[kind]
         wires.copy(kvf.at[kind], kvz.at[kind], kbase + kind * 3 + 2, zpair)
 
@@ -351,13 +401,13 @@
         qpt[kind, g] = dot(tokens[rows(0), :], weight[...])
 
     def q_across(kind):
-        wires.arrived(qr.at[kind, 0], qbase + kind * 3, sibling)
+        wires.arrived(qr.at[kind, 0], qbase + kind * 3)
         qpt[kind, 0] = qpt[kind, 0] + qr[kind, 0]
         wires.copy(qpt.at[kind, 0], qe.at[kind], qbase + kind * 3 + 2, ypair)
 
     def q_final(kind):
-        wires.arrived(qr.at[kind, 1], qbase + kind * 3 + 1, sibling)
-        wires.arrived(qe.at[kind], qbase + kind * 3 + 2, ypair)
+        wires.arrived(qr.at[kind, 1], qbase + kind * 3 + 1)
+        wires.arrived(qe.at[kind], qbase + kind * 3 + 2)
         total = qpt[kind, 1] + qr[kind, 1] + qe[kind]
         if kind == 0:
             total = total + 2.0 * dot(low[:, pl.ds(0, 64)], rq[...])
@@ -396,25 +446,24 @@
     ystep(1, 0)
     zstep(0, 1)
     xstep(0, 0)
-    xstep(0, 1)
     ystep(0, 2)
     ystep(0, 3)
+    xstep(0, 1)
     ystep(1, 1)
     xstep(0, 2)
     xstep(0, 3)
-    zstep(0, 2)
     ystep(1, 2)
     xstep(1, 0)
-    piece = scatter_sum(wires, me, "tensor", lowl, lbase)
-    lowg[me.t] = piece
-    gbase = gather_start(wires, me, "tensor", lowg)
+    zstep(0, 2)
+    lowg[me.t] = scatter_sum(wires, "tensor", lowl, lslot)
+    gslot = gather_start(wires, me, "tensor", lowg)
+    ystep(1, 3)
     xstep(1, 1)
-    ystep(1, 3)
     zstep(0, 3)
+    xstep(1, 2)
     zfirst(1, 0)
     zfirst(1, 1)
-    xstep(1, 2)
-    gather_wait(wires, me, "tensor", lowg, gbase)
+    gather_wait(wires, "tensor", lowg, gslot)
     for i in range(NT):
         flat[pl.ds(12 * i, 12), :] = lowg[i]
     low[...] = flat[...].astype(BF16)
@@ -425,24 +474,20 @@
         xend(0, j)
     kv_partial(0)
     xstep(1, 3)
-    zstep(1, 1)
     kv_across(0)
     xend(1, 0)
     xend(1, 1)
     q_partial(0, 0)
-    zstep(1, 2)
     kv_pieces(0)
+    zstep(1, 1)
     q_across(0)
-    zstep(1, 3)
     xend(1, 2)
     xend(1, 3)
     q_partial(0, 1)
-    zstep(1, 4)
-    wires.arrived(kvz.at[0], kbase + 2, zpair)
+    wires.arrived(kvz.at[0], kbase + 2)
     pair = [heads_of(0, s) for s in range(2)]
-    for d in range(1, 4):
-        theirs = pl.ds(pl.multiple_of(lax.rem(quarter + 4 - d, 4) * 32, 32), 32)
-        wires.arrived(rvh.at[theirs], vbase + d - 1, ypair)
+    wires.arrived(rvh.at[pl.ds(0, 96)], vslot)
+    zstep(1, 2)
     q_final(0)
 
     signs = [2.0 * flags[i].astype(F32) - 1.0 for i in range(2)]
@@ -484,28 +529,27 @@
     total_v = sum(dot_tn(part, lows2[s]) for s in range(2) for part in grads_v[s])
     for q in range(4):
         us[q] = 2.0 * total_v[q * 32 : (q + 1) * 32]
-    ubase = wires.slots(3)
+    uslot, usender = wires.slots(), wires.sender(us.at[pl.ds(0, 3)])
     for d, peer in enumerate(quarters):
-        wires.copy(us.at[lax.rem(quarter + d + 1, 4)], ul.at[quarter], ubase + d, peer)
+        wires.copy(us.at[lax.rem(quarter + d + 1, 4)], ul.at[quarter], uslot, peer, usender)
     ul[quarter] = us[quarter]
     for h in range(2):
         total_q = sum(dot_tn(lows2[s], grads_q[h][s]) for s in range(2))
         upf[pl.ds(h * 64, 64), :] = 2.0 * total_q[:64]
 
+    zstep(1, 3)
+    rows_g[me.t] = scatter_sum(wires, "tensor", rows_l, rbase)
+    gbase = gather_start(wires, me, "tensor", rows_g)
+    zstep(1, 4)
     kv_partial(1)
     q_partial(1, 0)
-    rows_g[me.t] = scatter_sum(wires, me, "tensor", rows_l, rbase)
-    gbase = gather_start(wires, me, "tensor", rows_g)
-    kv_across(1)
-    q_across(1)
     q_partial(1, 1)
-    for d in range(1, 4):
-        wires.arrived(ul.at[lax.rem(quarter + 4 - d, 4)], ubase + d - 1, ypair)
+    wires.arrived(ul.at[pl.ds(0, 3)], uslot)
     upf[pl.ds(128, 32), :] = ul[0] + ul[1] + ul[2] + ul[3]
     for i in range(NF):
         ups_s[i] = upf[pl.ds(5 * i, 5), :]
     upbase = scatter_start(wires, me, "fsdp", ups_s, ups_l)
-    gather_wait(wires, me, "tensor", rows_g, gbase)
+    gather_wait(wires, "tensor", rows_g, gbase)
     for i in range(NT):
         flat[pl.ds(12 * i, 12), :] = rows_g[i]
     down = 2.0 * dot_tn(flat[...].astype(BF16), xp[...])
@@ -513,14 +557,16 @@
         for j in range(4):
             gs[i * 4 + j] = down[i * 16 : (i + 1) * 16, j * 128 : (j + 1) * 128].astype(BF16)
     dbase = scatter_start(wires, me, "fsdp", gs, gl)
+    kv_across(1)
+    q_across(1)
+    ups[me.f] = scatter_sum(wires, "fsdp", ups_l, upbase)
+    upgather = gather_start(wires, me, "fsdp", ups)
+    grad[me.f] = scatter_sum(wires, "fsdp", gl, dbase).astype(BF16)
+    downgather = gather_start(wires, me, "fsdp", grad)
     kv_pieces(1)
     q_final(1)
-    ups[me.f] = scatter_sum(wires, me, "fsdp", ups_l, upbase)
-    upgather = gather_start(wires, me, "fsdp", ups)
-    grad[me.f] = scatter_sum(wires, me, "fsdp", gl, dbase).astype(BF16)
-    downgather = gather_start(wires, me, "fsdp", grad)
-
-    wires.arrived(kvz.at[1], kbase + 5, zpair)
+
+    wires.arrived(kvz.at[1], kbase + 5)
     for s in range(2):
         at = pl.ds(s * SEQ, SEQ)
         key, value = heads_of(1, s)
@@ -528,24 +574,24 @@
         for h in range(2):
             ctx[at, pl.ds(h * HD, HD)] = context[h * SEQ : (h + 1) * SEQ]
 
-    gather_wait(wires, me, "fsdp", ups, upgather)
+    gather_wait(wires, "fsdp", ups, upgather)
     for i in range(NF):
         upf[pl.ds(5 * i, 5), :] = ups[i]
     for h in range(2):
         up_q[:, pl.ds(h * 128, 128)] = upf[pl.ds(h * 64, 64), :]
     up_vt[...] = upf[pl.ds(128, 32), pl.ds(64, 64)]
-    gather_wait(wires, me, "fsdp", grad, downgather)
+    gather_wait(wires, "fsdp", grad, downgather)
     for i in range(8):
         target = qd_t if i < 4 else vd_t
         for j in range(4):
             target[pl.ds((i % 4) * 16, 16), pl.ds(j * 128, 128)] = grad[i * 4 + j].astype(F32)
-    for near in maybe:
-
-        @pl.when(yl != yl_d)
-        def _(near=near):
-            near.wait_send()
+    @pl.when(jnp.logical_not(inner))
+    def _():
+        for copy in passed:
+            copy.wait_send()
 
     wires.drain()
+    assert wires.sent <= 64 and wires.got <= 96, (wires.sent, wires.got)
 
 
 def tables():
@@ -612,9 +658,9 @@
             vm((160, 128), F32),
             *[vm((NF, 5, 128), F32)] * 3,
             *[vm((NF, 16, 128), BF16)] * 3,
-            pltpu.SemaphoreType.DMA((300,)),
-            pltpu.SemaphoreType.DMA((300,)),
-            pltpu.SemaphoreType.DMA((2,)),
+            pltpu.SemaphoreType.DMA((64,)),
+            pltpu.SemaphoreType.DMA((96,)),
+            pltpu.SemaphoreType.DMA((4,)),
         ],
         compiler_params=pltpu.CompilerParams(collective_id=0, has_side_effects=True),
         name="one_step",

time: 104 us -> 97.7 us (0.939)
  Pallas kernels: 98.5 us -> 92.1 us
    pallas_call x1, Pallas kernels: 98.5 us -> 92.1 us  [shards(): pl.pallas_call(one_step, out_shape=(shape((TOK, 256), BF16), shape((64, 5...]
where the time goes in v3:
time: 97.7 us; the launch traced here: 97.4 us
  Pallas kernels  92.1 us (94%)
  local copies, waits for them, and re-layouts  4.71 us (5%)
    pallas_call x1, Pallas kernels, shards(): pl.pallas_call(one_step, out_shape=(shape((TOK, 256), BF16), shape((64, 5...  92.1 us
    unnamed x13, local copies, waits for them, and re-layouts  4.71 us

profile of v3, /device:TPU:1, one launch (start us, length us, event | category | flops | bytes accessed | tf_op | source)
XLA Modules:
  0.0 97.4 jit_solution(5817272597645446149)
XLA Ops:
  0.6 92.1 %one_step.1 = (bf16[192,256]{1,0:T(8,128)(2,1)}, f32[64,512]{1,0:T(8,128)}, f32[64,512]{1,0:T(8,128)}, f32[64,256]{1,0:T(8,128)}, f32[32,64]{1,0:T(8,128)}) custom-call(bf16[192,512]{1,0:T(8,128)(2,1)} %xp.1, bf16[192,512]{1,0:T(8,128)(2,1)} %xr.1, bf16[192,256]{1,0:T(8,128)(2,1)} %cot.1, bf16[256,256]{1,0:T(8,128)(2,1)} %wq.1, bf16[32,256]{1,0:T(8,128)(2,1)} %bitcast.12, ...), custom_call_target="tpu_custom_call" | custom-call | tf_op jit(solution)/shard_map/one_step/pallas_call | solution.py:630
  92.7 0.0 copy-start.1
  92.7 1.6 %copy.26 = bf16[192,256]{1,0:T(8,128)(2,1)} copy(bf16[192,256]{1,0:T(8,128)(2,1)} %get-tuple-element.20) | data formatting | bytes 196608
  94.3 0.0 copy-done.1
  94.3 0.0 copy-start
  94.3 0.7 copy.27
  95.0 0.3 copy-done
  95.2 0.0 copy-start.2
  95.3 0.7 copy.28
  95.9 0.2 copy-done.2
  96.1 0.0 copy-start.3
  96.1 0.6 copy.29
  96.7 0.1 copy-done.3
  96.8 0.6 copy.30
Async XLA Ops:
  92.7 1.6 %copy-start.1 = (f32[64,512]{1,0:T(8,128)S(1)}, f32[64,512]{1,0:T(8,128)}, u32[]{:S(2)}) copy-start(f32[64,512]{1,0:T(8,128)} %get-tuple-element.11) | copy-start | bytes 393220
  94.3 1.0 copy-start
  95.2 0.9 copy-start.2
  96.1 0.7 copy-start.3

commit v4 on v3

--- a/solution.py
+++ b/solution.py
@@ -159,10 +159,10 @@
 
 def one_step(
     xp, xr, cot, wq, wkt, wvt, qdt, vdt, rq, rvt, cosine, sine, plen, rlen, flags, ratios,
-    ctx, qd_t, vd_t, up_q, up_vt,
+    ctx, grad, upf,
     xg, wgq, wgk, kvo, rvx, rvh, low, flat, lows, lowl, lowg,
     kvp, kvs, kvr, kve, kvf, kvz, qpt, qs, qr, qe, query,
-    rows_s, rows_l, rows_g, us, ul, upf, ups_s, ups_l, ups, gs, gl, grad, send, recv, local,
+    rows_s, rows_l, rows_g, us, ul, ups_s, ups_l, ups, gs, gl, send, recv, local,
 ):
     me = Place()
     c, z, x, yh, yl = me.c, me.z, me.x, me.yh, me.yl
@@ -203,10 +203,6 @@
     rvx[pl.ds(pl.multiple_of(yl * 64 + 32, 32), 32), :] = rvt[...]
     my_quarter = pl.ds(pl.multiple_of(quarter * 32, 32), 32)
     rvh[my_quarter, :] = rvt[...]
-    down_t = jnp.concatenate([qdt[...], vdt[...]], axis=0)
-    flat[...] = dot_nt(xp[...], down_t)
-    for i in range(NT):
-        lows[i] = flat[pl.ds(12 * i, 12), :]
     met(count)
 
     m_own = yh // 2
@@ -330,6 +326,10 @@
     sib_send(0)
     zfirst(0, 0)
     y_sends(1, wq)
+    down_t = jnp.concatenate([qdt[...], vdt[...]], axis=0)
+    flat[...] = dot_nt(xp[...], down_t)
+    for i in range(NT):
+        lows[i] = flat[pl.ds(12 * i, 12), :]
     lslot = scatter_start(wires, me, "tensor", lows, lowl)
     vslot, vsender = wires.slots(), wires.sender(rvh.at[pl.ds(0, 96)])
     for peer in quarters:
@@ -447,8 +447,10 @@
     zstep(0, 1)
     xstep(0, 0)
     ystep(0, 2)
+    xstep(0, 1)
     ystep(0, 3)
-    xstep(0, 1)
+    zfirst(1, 0)
+    zfirst(1, 1)
     ystep(1, 1)
     xstep(0, 2)
     xstep(0, 3)
@@ -460,34 +462,33 @@
     ystep(1, 3)
     xstep(1, 1)
     zstep(0, 3)
+    zstep(1, 1)
     xstep(1, 2)
-    zfirst(1, 0)
-    zfirst(1, 1)
     gather_wait(wires, "tensor", lowg, gslot)
     for i in range(NT):
         flat[pl.ds(12 * i, 12), :] = lowg[i]
     low[...] = flat[...].astype(BF16)
+    for j in range(4):
+        xend(0, j)
     zstep(0, 4)
     for copy in own:
         copy.wait()
-    for j in range(4):
-        xend(0, j)
     kv_partial(0)
-    xstep(1, 3)
-    kv_across(0)
     xend(1, 0)
     xend(1, 1)
+    kv_across(0)
     q_partial(0, 0)
+    xstep(1, 3)
+    q_across(0)
+    zstep(1, 2)
     kv_pieces(0)
-    zstep(1, 1)
-    q_across(0)
     xend(1, 2)
     xend(1, 3)
     q_partial(0, 1)
+    zstep(1, 3)
     wires.arrived(kvz.at[0], kbase + 2)
     pair = [heads_of(0, s) for s in range(2)]
     wires.arrived(rvh.at[pl.ds(0, 96)], vslot)
-    zstep(1, 2)
     q_final(0)
 
     signs = [2.0 * flags[i].astype(F32) - 1.0 for i in range(2)]
@@ -537,7 +538,6 @@
         total_q = sum(dot_tn(lows2[s], grads_q[h][s]) for s in range(2))
         upf[pl.ds(h * 64, 64), :] = 2.0 * total_q[:64]
 
-    zstep(1, 3)
     rows_g[me.t] = scatter_sum(wires, "tensor", rows_l, rbase)
     gbase = gather_start(wires, me, "tensor", rows_g)
     zstep(1, 4)
@@ -577,21 +577,25 @@
     gather_wait(wires, "fsdp", ups, upgather)
     for i in range(NF):
         upf[pl.ds(5 * i, 5), :] = ups[i]
-    for h in range(2):
-        up_q[:, pl.ds(h * 128, 128)] = upf[pl.ds(h * 64, 64), :]
-    up_vt[...] = upf[pl.ds(128, 32), pl.ds(64, 64)]
     gather_wait(wires, "fsdp", grad, downgather)
+    @pl.when(jnp.logical_not(inner))
+    def _():
+        for copy in passed:
+            copy.wait_send()
+
+    wires.drain()
+    assert wires.sent <= 64 and wires.got <= 96, (wires.sent, wires.got)
+
+
+def hand_out(context, grad, ups, ctx, qd_t, vd_t, up_q, up_vt):
+    ctx[...] = context[...]
     for i in range(8):
         target = qd_t if i < 4 else vd_t
         for j in range(4):
             target[pl.ds((i % 4) * 16, 16), pl.ds(j * 128, 128)] = grad[i * 4 + j].astype(F32)
-    @pl.when(jnp.logical_not(inner))
-    def _():
-        for copy in passed:
-            copy.wait_send()
-
-    wires.drain()
-    assert wires.sent <= 64 and wires.got <= 96, (wires.sent, wires.got)
+    for h in range(2):
+        up_q[:, pl.ds(h * 128, 128)] = ups[pl.ds(h * 64, 64), :]
+    up_vt[...] = ups[pl.ds(128, 32), pl.ds(64, 64)]
 
 
 def tables():
@@ -627,17 +631,15 @@
 ):
     cosine, sine = tables()
     vm = pltpu.VMEM
-    context, qd_t, vd_t, query_up, up_vt = pl.pallas_call(
+    context, grad, ups = pl.pallas_call(
         one_step,
         out_shape=(
             shape((TOK, 256), BF16),
-            shape((64, 512), F32),
-            shape((64, 512), F32),
-            shape((64, 256), F32),
-            shape((32, 64), F32),
+            shape((NF, 16, 128), BF16),
+            shape((160, 128), F32),
         ),
         in_specs=[VM] * 12 + [SM] * 4,
-        out_specs=(VM,) * 5,
+        out_specs=(VM,) * 3,
         scratch_shapes=[
             vm((2, 384, 2048), BF16),
             vm((2, 2048, 256), BF16),
@@ -655,9 +657,8 @@
             *[vm((2, TOK, 256), F32)] * 2,
             *[vm((NT, 12, 128), F32)] * 3,
             *[vm((4, 32, 128), F32)] * 2,
-            vm((160, 128), F32),
             *[vm((NF, 5, 128), F32)] * 3,
-            *[vm((NF, 16, 128), BF16)] * 3,
+            *[vm((NF, 16, 128), BF16)] * 2,
             pltpu.SemaphoreType.DMA((64,)),
             pltpu.SemaphoreType.DMA((96,)),
             pltpu.SemaphoreType.DMA((4,)),
@@ -669,6 +670,19 @@
         query_down.T, value_down.T, query_raise_factor, value_raise_factor.T, cosine, sine,
         policy_lengths, reference_lengths, chosen_flags, log_ratios,
     )
+    context, qd_t, vd_t, query_up, up_vt = pl.pallas_call(
+        hand_out,
+        out_shape=(
+            shape((TOK, 256), BF16),
+            shape((64, 512), F32),
+            shape((64, 512), F32),
+            shape((64, 256), F32),
+            shape((32, 64), F32),
+        ),
+        in_specs=[VM] * 3,
+        out_specs=(VM,) * 5,
+        name="hand_out",
+    )(context, grad, ups)
     return context, qd_t.T, vd_t.T, query_up, up_vt.T
 
 

time: 97.7 us -> 93.2 us (0.954)
  local copies, waits for them, and re-layouts: 4.71 us -> 0 us
    unnamed x13 -> x0, local copies, waits for them, and re-layouts: 4.71 us -> none
    pallas_call x1 -> x2, Pallas kernels: 92.1 us -> 92.4 us  [the longest x1 90.7 us: shards(): pl.pallas_call(one_step, out_shape=(shape((TOK, 256), BF16), shape((NF, 1...]
where the time goes in v4:
time: 93.2 us; the launch traced here: 93.1 us
  Pallas kernels  92.4 us (99%)
    pallas_call x1, Pallas kernels, shards(): pl.pallas_call(one_step, out_shape=(shape((TOK, 256), BF16), shape((NF, 1...  90.7 us

profile of v4, /device:TPU:1, one launch (start us, length us, event | category | flops | bytes accessed | tf_op | source)
XLA Modules:
  0.0 93.1 jit_solution(13246048220864876766)
XLA Ops:
  0.6 90.7 %one_step.1 = (bf16[192,256]{1,0:T(8,128)(2,1)}, bf16[32,16,128]{2,1,0:T(8,128)(2,1)}, f32[160,128]{1,0:T(8,128)}) custom-call(bf16[192,512]{1,0:T(8,128)(2,1)} %xp.1, bf16[192,512]{1,0:T(8,128)(2,1)} %xr.1, bf16[192,256]{1,0:T(8,128)(2,1)} %cot.1, bf16[256,256]{1,0:T(8,128)(2,1)} %wq.1, bf16[32,256]{1,0:T(8,128)(2,1)} %bitcast.10, ...), custom_call_target="tpu_custom_call" | custom-call | tf_op jit(solution)/shard_map/one_step/pallas_call | solution.py:634
  91.3 1.8 %hand_out.1 = (bf16[192,256]{1,0:T(8,128)(2,1)}, f32[64,512]{1,0:T(8,128)}, f32[64,512]{1,0:T(8,128)}, f32[64,256]{1,0:T(8,128)}, f32[32,64]{1,0:T(8,128)}) custom-call(bf16[192,256]{1,0:T(8,128)(2,1)} %get-tuple-element.13.context, bf16[32,16,128]{2,1,0:T(8,128)(2,1)} %get-tuple-element.14.grad, f32[160,128]{1,0:T(8,128)} %get-tuple-element.15.ups), custom_call_target="tpu_custom_call" | custom-call | tf_op jit(solution)/shard_map/hand_out/pallas_call | solution.py:673

commit v5 on v4

--- a/solution.py
+++ b/solution.py
@@ -19,6 +19,8 @@
 SM = pl.BlockSpec(memory_space=pltpu.SMEM)
 NT = 16
 NF = 32
+SENT = 37
+GOT = 96
 
 
 def dot(a, b):
@@ -584,7 +586,7 @@
             copy.wait_send()
 
     wires.drain()
-    assert wires.sent <= 64 and wires.got <= 96, (wires.sent, wires.got)
+    assert (wires.sent, wires.got) == (SENT, GOT), (wires.sent, wires.got)
 
 
 def hand_out(context, grad, ups, ctx, qd_t, vd_t, up_q, up_vt):
@@ -659,8 +661,8 @@
             *[vm((4, 32, 128), F32)] * 2,
             *[vm((NF, 5, 128), F32)] * 3,
             *[vm((NF, 16, 128), BF16)] * 2,
-            pltpu.SemaphoreType.DMA((64,)),
-            pltpu.SemaphoreType.DMA((96,)),
+            pltpu.SemaphoreType.DMA((SENT,)),
+            pltpu.SemaphoreType.DMA((GOT,)),
             pltpu.SemaphoreType.DMA((4,)),
         ],
         compiler_params=pltpu.CompilerParams(collective_id=0, has_side_effects=True),

time: 93.2 us -> 93 us (level)
  no operation moved by 1% of the time
where the time goes in v5:
time: 93 us; the launch traced here: 92.8 us
  Pallas kernels  92.2 us (99%)
    pallas_call x1, Pallas kernels, shards(): pl.pallas_call(one_step, out_shape=(shape((TOK, 256), BF16), shape((NF, 1...  90.4 us

profile of v5, /device:TPU:1, one launch (start us, length us, event | category | flops | bytes accessed | tf_op | source)
XLA Modules:
  0.0 92.8 jit_solution(8894586500096937506)
XLA Ops:
  0.6 90.4 %one_step.1 = (bf16[192,256]{1,0:T(8,128)(2,1)}, bf16[32,16,128]{2,1,0:T(8,128)(2,1)}, f32[160,128]{1,0:T(8,128)}) custom-call(bf16[192,512]{1,0:T(8,128)(2,1)} %xp.1, bf16[192,512]{1,0:T(8,128)(2,1)} %xr.1, bf16[192,256]{1,0:T(8,128)(2,1)} %cot.1, bf16[256,256]{1,0:T(8,128)(2,1)} %wq.1, bf16[32,256]{1,0:T(8,128)(2,1)} %bitcast.10, ...), custom_call_target="tpu_custom_call" | custom-call | tf_op jit(solution)/shard_map/one_step/pallas_call | solution.py:636
  91.1 1.8 %hand_out.1 = (bf16[192,256]{1,0:T(8,128)(2,1)}, f32[64,512]{1,0:T(8,128)}, f32[64,512]{1,0:T(8,128)}, f32[64,256]{1,0:T(8,128)}, f32[32,64]{1,0:T(8,128)}) custom-call(bf16[192,256]{1,0:T(8,128)(2,1)} %get-tuple-element.13.context, bf16[32,16,128]{2,1,0:T(8,128)(2,1)} %get-tuple-element.14.grad, f32[160,128]{1,0:T(8,128)} %get-tuple-element.15.ups), custom_call_target="tpu_custom_call" | custom-call | tf_op jit(solution)/shard_map/hand_out/pallas_call | solution.py:675
